TPU v7x, 32 devices: a whole 2x2x4 slice. The times are simulated.
32 devices in a mesh: expert: 8 (over z, core), cuts: 4 (over y, x).
Axes of the slice: x: 2, y: 2, z: 4, core: 2. Of those that a mesh axis runs over, the one named last changes fastest.
Arguments:
- block_input: bfloat16 [8192, 1024], P(('expert', 'cuts')), may hold values from -6 to 6
- routes: int32 [8192], P(('expert', 'cuts')), may hold values from 0 to 31, as said below
- kept_mask: int32 [8192], P(('expert', 'cuts')), may hold values from 0 to 1, as said below
- w_qkv: bfloat16 [1024, 3072], P('cuts'), may hold values from -0.1875 to 0.1875
- w_attn_out: bfloat16 [1024, 1024], P('cuts'), may hold values from -1 to 1
- w_in: bfloat16 [1024, 4096], P('cuts'), may hold values from -0.1875 to 0.1875
- w_out: bfloat16 [4096, 1024], P('cuts'), may hold values from -0.1875 to 0.1875
- w_router: bfloat16 [1024, 32], P('cuts'), may hold values from -0.09375 to 0.09375
- w_mix: bfloat16 [1024, 2], P('cuts'), may hold values from -0.1875 to 0.1875
- gain_attn: bfloat16 [1024], P('cuts'), may hold values from 0.5 to 1.5
- gain_ffn: bfloat16 [1024], P('cuts'), may hold values from 0.5 to 1.5
- expert_in: bfloat16 [32, 1024, 4096], P('expert', None, 'cuts'), may hold values from -0.1875 to 0.1875
- expert_out: bfloat16 [32, 4096, 1024], P('expert', 'cuts'), may hold values from -6 to 6
- cotangent: bfloat16 [8192, 1024], P(('expert', 'cuts')), may hold values from -6 to 6
Outputs:
- block_out: bfloat16 [8192, 1024], P(('expert', 'cuts'))
- d_block_input: float32 [8192, 1024], P(('expert', 'cuts'))
- d_w_qkv: float32 [1024, 3072], P(('expert', 'cuts'))
- d_w_attn_out: float32 [1024, 1024], P(('expert', 'cuts'))
- d_w_in: float32 [1024, 4096], P(('expert', 'cuts'))
- d_w_out: float32 [4096, 1024], P(('expert', 'cuts'))
- d_w_router: float32 [1024, 32], P(('expert', 'cuts'))
- d_w_mix: float32 [1024, 2], P(('expert', 'cuts'))
- d_gain_attn: float32 [1024], P(('expert', 'cuts'))
- d_gain_ffn: float32 [1024], P(('expert', 'cuts'))
- d_expert_in: float32 [32, 1024, 4096], P('expert', None, 'cuts')
- d_expert_out: float32 [32, 4096, 1024], P('expert', 'cuts')
Inputs may be any that keep to these rules, and one draw needn't show every extreme that they name: `routes`: the expert of each token; a few experts are far more common than the rest. kept_mask is 1 exactly for the first 12 tokens of each expert within the rows of one device, in token order; on every device some expert fills all 12 of its slots.
All inputs are finite; a program needn't handle non-finite values.
Results may differ from a plain program's by a relative error of at most 0.017.
Values may be sent and summed in bfloat16 or wider, within the bound.
A program may use at most 320 MiB of HBM per device.

v0:
```python
from functools import partial

import jax
import jax.numpy as jnp
from jax import lax
from jax.sharding import PartitionSpec as P

H = 16
HD = 64


def layer_norm(values, gain):
    center = values - jnp.mean(values, axis=-1, keepdims=True)
    spread = jnp.mean(center * center, axis=-1, keepdims=True)
    return center * lax.rsqrt(spread + 1e-05) * gain


def contract_last(left, right):
    return lax.dot_general(
        left, right, (((1,), (1,)), ((), ())), preferred_element_type=jnp.float32
    )


def contract_first(left, right):
    return lax.dot_general(
        left, right, (((0,), (0,)), ((), ())), preferred_element_type=jnp.float32
    )


def softmax_rows(logits):
    shifted = logits - jnp.max(logits, axis=-1, keepdims=True)
    row_exp = jnp.exp(shifted)
    return row_exp / jnp.sum(row_exp, axis=-1, keepdims=True)


def route_gates(onehot, router_logits, mix_logits):
    router_p = softmax_rows(router_logits)
    return (jnp.sum(router_p * onehot, axis=1), softmax_rows(mix_logits))


def to_owners(rows, experts_here):
    owners = lax.axis_size("expert")
    grid = rows.reshape(owners, experts_here, -1, rows.shape[-1])
    moved = lax.all_to_all(grid, "expert", split_axis=0, concat_axis=2, tiled=True)
    return lax.all_gather(moved, "cuts", axis=2, tiled=True)[0]


def to_sources(partial_rows):
    summed = lax.psum_scatter(
        partial_rows[None].astype(jnp.bfloat16), "cuts", scatter_dimension=2, tiled=True
    )
    moved = lax.all_to_all(summed, "expert", split_axis=2, concat_axis=0, tiled=True)
    return moved.reshape(-1, moved.shape[-1])


def masked_scores(queries, key_rows, visible, scaling):
    scores = (
        jnp.einsum("qhd,khd->hqk", queries, key_rows, preferred_element_type=jnp.float32) * scaling
    )
    return jnp.where(visible[None], scores, -1e30)


def shards(
    block_input,
    routes,
    kept_mask,
    w_qkv,
    w_attn_out,
    w_in,
    w_out,
    w_router,
    w_mix,
    gain_attn,
    gain_ffn,
    expert_in,
    expert_out,
    cotangent,
):
    full = (
        lax.all_gather(w_qkv, "cuts", axis=0, tiled=True),
        lax.all_gather(w_attn_out, "cuts", axis=0, tiled=True),
        lax.all_gather(w_in, "cuts", axis=0, tiled=True),
        lax.all_gather(w_out, "cuts", axis=0, tiled=True),
        lax.all_gather(w_router, "cuts", axis=0, tiled=True),
        lax.all_gather(w_mix, "cuts", axis=0, tiled=True),
        lax.all_gather(gain_attn, "cuts", axis=0, tiled=True),
        lax.all_gather(gain_ffn, "cuts", axis=0, tiled=True),
    )
    qkv_full, attn_full, in_full, out_full, router_full, mixer_full, gain_one, gain_two = full
    tokens = block_input.shape[0]
    features = block_input.shape[1]
    scaling = HD ** (-0.5)
    per_group = H // 4
    offset = lax.axis_index("cuts") * tokens
    seq_len = tokens * lax.axis_size("cuts")
    experts_all = router_full.shape[1]
    experts_here = expert_in.shape[0]
    capacity = 3 * tokens // (2 * experts_all)
    inputs = block_input.astype(jnp.float32)
    normed, norm_one_pull = jax.vjp(layer_norm, inputs, gain_one.astype(jnp.float32))
    normed_low = normed.astype(jnp.bfloat16)
    joined = jnp.dot(normed_low, qkv_full, preferred_element_type=jnp.float32).astype(jnp.bfloat16)
    queries = joined[:, :features]
    key_rows = joined[:, features : 2 * features]
    value_rows = joined[:, 2 * features :]
    all_keys, all_values = (
        lax.all_gather(key_rows, "cuts", axis=0, tiled=True),
        lax.all_gather(value_rows, "cuts", axis=0, tiled=True),
    )
    q_heads = queries.reshape(tokens, H, HD)
    k_heads = all_keys.reshape(seq_len, H, HD)
    v_heads = all_values.reshape(seq_len, H, HD)
    row_pos = offset + jnp.arange(tokens, dtype=jnp.int32)
    col_pos = jnp.arange(seq_len, dtype=jnp.int32)
    visible = col_pos[None, :] <= row_pos[:, None]
    head_parts = []
    lse_parts = []
    for group_id in range(4):
        head_span = slice(group_id * per_group, (group_id + 1) * per_group)
        scores = masked_scores(q_heads[:, head_span], k_heads[:, head_span], visible, scaling)
        row_peak = jnp.max(scores, axis=-1, keepdims=True)
        row_exp = jnp.exp(scores - row_peak)
        row_total = jnp.sum(row_exp, axis=-1, keepdims=True)
        weights_p = (row_exp / row_total).astype(jnp.bfloat16)
        head_parts.append(
            jnp.einsum(
                "hqk,khd->qhd", weights_p, v_heads[:, head_span], preferred_element_type=jnp.float32
            )
        )
        lse_parts.append((row_peak + jnp.log(row_total))[:, :, 0])
    head_out = jnp.concatenate(head_parts, axis=1).reshape(tokens, features).astype(jnp.bfloat16)
    log_norm = jnp.concatenate(lse_parts, axis=0)
    hidden = inputs + jnp.dot(head_out, attn_full, preferred_element_type=jnp.float32)
    second_f, norm_two_pull = jax.vjp(layer_norm, hidden, gain_two.astype(jnp.float32))
    second = second_f.astype(jnp.bfloat16)
    up_proj = jnp.dot(second, in_full, preferred_element_type=jnp.float32)
    activ, gelu_pull = jax.vjp(jax.nn.gelu, up_proj)
    activ_low = activ.astype(jnp.bfloat16)
    dense = jnp.dot(activ_low, out_full, preferred_element_type=jnp.float32)
    onehot = (routes[:, None] == jnp.arange(experts_all, dtype=jnp.int32)[None, :]).astype(
        jnp.float32
    )
    router_logits = jnp.dot(second, router_full, preferred_element_type=jnp.float32)
    mix_logits = jnp.dot(second, mixer_full, preferred_element_type=jnp.float32)
    (gate, mixing), gates_pull = jax.vjp(partial(route_gates, onehot), router_logits, mix_logits)
    onehot_kept = onehot * kept_mask.astype(jnp.float32)[:, None]
    lower_tri = (jnp.arange(tokens)[:, None] >= jnp.arange(tokens)[None, :]).astype(jnp.bfloat16)
    running = jnp.dot(
        lower_tri, onehot_kept.astype(jnp.bfloat16), preferred_element_type=jnp.float32
    )
    slot_num = jnp.sum(onehot_kept * running, axis=1) - 1.0
    target = routes.astype(jnp.float32) * capacity + slot_num
    columns = jnp.arange(experts_all * capacity, dtype=jnp.int32).astype(jnp.float32)
    placer = ((columns[None, :] == target[:, None]) & (kept_mask[:, None] > 0)).astype(jnp.bfloat16)
    slots_in = contract_first(placer, second).astype(jnp.bfloat16)
    rows_in = to_owners(slots_in, experts_here)
    first = jnp.einsum("erd,edh->erh", rows_in, expert_in, preferred_element_type=jnp.float32)
    expert_act, expert_gelu_pull = jax.vjp(jax.nn.gelu, first)
    expert_low = expert_act.astype(jnp.bfloat16)
    partial_out = jnp.einsum(
        "erh,ehd->erd", expert_low, expert_out, preferred_element_type=jnp.float32
    )
    returned = to_sources(partial_out)
    picked = jnp.dot(placer, returned, preferred_element_type=jnp.float32)
    moe_val = gate[:, None] * picked
    result = hidden + mixing[:, 0:1] * dense + mixing[:, 1:2] * moe_val
    block_out = result.astype(jnp.bfloat16)
    grad = cotangent.astype(jnp.float32)
    d_mixing = jnp.stack([jnp.sum(grad * dense, axis=1), jnp.sum(grad * moe_val, axis=1)], axis=1)
    d_dense = (grad * mixing[:, 0:1]).astype(jnp.bfloat16)
    d_moe = grad * mixing[:, 1:2]
    d_gate = jnp.sum(d_moe * picked, axis=1)
    d_picked = (d_moe * gate[:, None]).astype(jnp.bfloat16)
    d_router_logits, d_mix_logits = gates_pull((d_gate, d_mixing))
    d_router_low = d_router_logits.astype(jnp.bfloat16)
    d_mix_low = d_mix_logits.astype(jnp.bfloat16)
    d_activ = contract_last(d_dense, out_full)
    g_out = contract_first(activ_low, d_dense)
    d_up = gelu_pull(d_activ)[0].astype(jnp.bfloat16)
    g_in = contract_first(second, d_up)
    g_router = contract_first(second, d_router_low)
    g_mix = contract_first(second, d_mix_low)
    d_slots = contract_first(placer, d_picked).astype(jnp.bfloat16)
    d_rows = to_owners(d_slots, experts_here)
    d_expert_act = jnp.einsum(
        "erd,ehd->erh", d_rows, expert_out, preferred_element_type=jnp.float32
    )
    g_expert_out = jnp.einsum(
        "erh,erd->ehd", expert_low, d_rows, preferred_element_type=jnp.float32
    )
    d_first = expert_gelu_pull(d_expert_act)[0].astype(jnp.bfloat16)
    g_expert_in = jnp.einsum("erd,erh->edh", rows_in, d_first, preferred_element_type=jnp.float32)
    d_rows_in = jnp.einsum("erh,edh->erd", d_first, expert_in, preferred_element_type=jnp.float32)
    d_back = to_sources(d_rows_in)
    d_second = (
        contract_last(d_up, in_full)
        + contract_last(d_router_low, router_full)
        + contract_last(d_mix_low, mixer_full)
    )
    d_second = d_second + jnp.dot(placer, d_back, preferred_element_type=jnp.float32)
    d_hidden_norm, g_gain_two = norm_two_pull(d_second)
    d_hidden = grad + d_hidden_norm
    d_attn = d_hidden.astype(jnp.bfloat16)
    g_attn_out = contract_first(head_out, d_attn)
    d_heads = contract_last(d_attn, attn_full).astype(jnp.bfloat16)
    dh_heads = d_heads.reshape(tokens, H, HD)
    dq_parts = []
    dk_parts = []
    dv_parts = []
    for group_id in range(4):
        head_span = slice(group_id * per_group, (group_id + 1) * per_group)
        scores = masked_scores(q_heads[:, head_span], k_heads[:, head_span], visible, scaling)
        soft_p = jnp.exp(scores - log_norm[head_span][:, :, None])
        d_soft = jnp.einsum(
            "qhd,khd->hqk",
            dh_heads[:, head_span],
            v_heads[:, head_span],
            preferred_element_type=jnp.float32,
        )
        delta = jnp.sum(soft_p * d_soft, axis=-1)
        d_scores = (soft_p * (d_soft - delta[:, :, None])).astype(jnp.bfloat16)
        dq_parts.append(
            jnp.einsum(
                "hqk,khd->qhd", d_scores, k_heads[:, head_span], preferred_element_type=jnp.float32
            )
            * scaling
        )
        dv_parts.append(
            jnp.einsum(
                "hqk,qhd->khd",
                soft_p.astype(jnp.bfloat16),
                dh_heads[:, head_span],
                preferred_element_type=jnp.float32,
            )
        )
        dk_parts.append(
            jnp.einsum(
                "hqk,qhd->khd", d_scores, q_heads[:, head_span], preferred_element_type=jnp.float32
            )
            * scaling
        )
    d_query = jnp.concatenate(dq_parts, axis=1).reshape(tokens, features).astype(jnp.bfloat16)
    key_total = jnp.concatenate(dk_parts, axis=1).reshape(seq_len, features)
    value_total = jnp.concatenate(dv_parts, axis=1).reshape(seq_len, features)
    d_keys, d_values = (
        lax.psum_scatter(
            key_total.astype(jnp.bfloat16), "cuts", scatter_dimension=0, tiled=True
        ).astype(jnp.float32),
        lax.psum_scatter(
            value_total.astype(jnp.bfloat16), "cuts", scatter_dimension=0, tiled=True
        ).astype(jnp.float32),
    )
    d_joined = jnp.concatenate(
        [d_query, d_keys.astype(jnp.bfloat16), d_values.astype(jnp.bfloat16)], axis=1
    )
    g_qkv = contract_first(normed_low, d_joined)
    d_normed = contract_last(d_joined, qkv_full)
    d_input_norm, g_gain_one = norm_one_pull(d_normed)
    d_block_input = d_hidden + d_input_norm
    all_sums = (
        lax.psum_scatter(g_qkv, ("expert", "cuts"), scatter_dimension=0, tiled=True),
        lax.psum_scatter(g_attn_out, ("expert", "cuts"), scatter_dimension=0, tiled=True),
        lax.psum_scatter(g_in, ("expert", "cuts"), scatter_dimension=0, tiled=True),
        lax.psum_scatter(g_out, ("expert", "cuts"), scatter_dimension=0, tiled=True),
        lax.psum_scatter(g_router, ("expert", "cuts"), scatter_dimension=0, tiled=True),
        lax.psum_scatter(g_mix, ("expert", "cuts"), scatter_dimension=0, tiled=True),
        lax.psum_scatter(g_gain_one, ("expert", "cuts"), scatter_dimension=0, tiled=True),
        lax.psum_scatter(g_gain_two, ("expert", "cuts"), scatter_dimension=0, tiled=True),
    )
    s_qkv, s_attn_out, s_in, s_out, s_router, s_mix, s_gain_one, s_gain_two = all_sums
    return (
        block_out,
        d_block_input,
        s_qkv,
        s_attn_out,
        s_in,
        s_out,
        s_router,
        s_mix,
        s_gain_one,
        s_gain_two,
        g_expert_in,
        g_expert_out,
    )


def solution(mesh):
    placed = (
        P(("expert", "cuts"), None),
        P(("expert", "cuts")),
        P(("expert", "cuts")),
        P("cuts", None),
        P("cuts", None),
        P("cuts", None),
        P("cuts", None),
        P("cuts", None),
        P("cuts", None),
        P("cuts"),
        P("cuts"),
        P("expert", None, "cuts"),
        P("expert", "cuts", None),
        P(("expert", "cuts"), None),
    )
    return jax.shard_map(
        shards,
        mesh=mesh,
        in_specs=placed,
        out_specs=(
            P(("expert", "cuts"), None),
            P(("expert", "cuts"), None),
            P(("expert", "cuts"), None),
            P(("expert", "cuts"), None),
            P(("expert", "cuts"), None),
            P(("expert", "cuts"), None),
            P(("expert", "cuts"), None),
            P(("expert", "cuts"), None),
            P(("expert", "cuts")),
            P(("expert", "cuts")),
            P("expert", None, "cuts"),
            P("expert", "cuts", None),
        ),
        check_vma=False,
    )
```

profile of v0, /device:TPU:0, one launch (start us, length us, event | category | flops | bytes accessed | tf_op | source)
XLA Modules:
  0.0 2026.0 jit_solution(17552874963188715409)
XLA Ops:
  20.9 61.7 %all-gather.11.cloned.1.call-done = bf16[1024,3072]{1,0:T(8,128)(2,1)} async-done(((bf16[256,3072]{1,0:T(8,128)(2,1)}), bf16[1024,3072]{1,0:T(8,128)(2,1)}) %all-gather.11.cloned.1.call-update) | async-done | bytes 6291472 | tf_op jit(solution)/shard_map/all_gather | solution.py:80
  98.8 25.2 %all-gather.15.cloned.1.call-done = bf16[1024,1024]{1,0:T(8,128)(2,1)} async-done(((bf16[256,1024]{1,0:T(8,128)(2,1)}), bf16[1024,1024]{1,0:T(8,128)(2,1)}) %all-gather.15.cloned.1.call-update) | async-done | bytes 2097168 | tf_op jit(solution)/shard_map/all_gather | solution.py:107
  135.6 26.0 %all-gather.13.cloned.1.call-done = bf16[1024,1024]{1,0:T(8,128)(2,1)} async-done(((bf16[256,1024]{1,0:T(8,128)(2,1)}), bf16[1024,1024]{1,0:T(8,128)(2,1)}) %all-gather.13.cloned.1.call-update) | async-done | bytes 2097168 | tf_op jit(solution)/shard_map/all_gather | solution.py:108
  175.0 23.6 %all-gather.17.cloned.1.call-done = bf16[1024,1024]{1,0:T(8,128)(2,1)} async-done(((bf16[256,1024]{1,0:T(8,128)(2,1)}), bf16[1024,1024]{1,0:T(8,128)(2,1)}) %all-gather.17.cloned.1.call-update) | async-done | bytes 2097168 | tf_op jit(solution)/shard_map/all_gather | solution.py:81
  205.1 25.3 %all_to_all.66 = bf16[8,4,12,1024]{3,1,2,0:T(4,128)(2,1)S(1)} all-to-all(bf16[8,4,12,1024]{3,1,2,0:T(4,128)(2,1)S(1)} %copy.63), channel_id=1, replica_groups=mesh['expert'=8,'cuts'=4] {'expert'}, dimensions={0} | all-to-all | bytes 1572864 | tf_op jit(solution)/shard_map/all_to_all | solution.py:44
  254.5 23.4 %all_to_all.67 = bf16[8,4,12,1024]{3,1,2,0:T(4,128)(2,1)S(1)} all-to-all(bf16[8,4,12,1024]{3,1,2,0:T(4,128)(2,1)S(1)} %copy.67), channel_id=1, replica_groups=mesh['expert'=8,'cuts'=4] {'expert'}, dimensions={0} | all-to-all | bytes 1572864 | tf_op jit(solution)/shard_map/all_to_all | solution.py:44
  291.4 29.5 %all-gather.25.cloned.1.call-done = bf16[1,4,384,1024]{3,2,1,0:T(8,128)(2,1)} async-done(((bf16[1,4,96,1024]{3,2,1,0:T(8,128)(2,1)}), bf16[1,4,384,1024]{3,2,1,0:T(8,128)(2,1)}) %all-gather.25.cloned.1.call-update) | async-done | bytes 3145744 | tf_op jit(solution)/shard_map/all_gather | solution.py:45
  321.0 11.1 fusion.6
  355.2 55.1 %all-gather.19.cloned.1.call-done = bf16[1024,4096]{1,0:T(8,128)(2,1)} async-done(((bf16[256,4096]{1,0:T(8,128)(2,1)}), bf16[1024,4096]{1,0:T(8,128)(2,1)}) %all-gather.19.cloned.1.call-update) | async-done | bytes 8388624 | tf_op jit(solution)/shard_map/all_gather | solution.py:82
  418.0 81.7 %all-gather.21.cloned.1.call-done = bf16[4096,1024]{1,0:T(8,128)(2,1)} async-done(((bf16[1024,1024]{1,0:T(8,128)(2,1)}), bf16[4096,1024]{1,0:T(8,128)(2,1)}) %all-gather.21.cloned.1.call-update) | async-done | bytes 8388624 | tf_op jit(solution)/shard_map/all_gather | solution.py:83
  499.7 12.4 fusion.13
  512.1 34.5 %reduce-scatter.15.cloned.1.call-done = bf16[1,4,96,1024]{3,2,1,0:T(8,128)(2,1)} async-done(((bf16[1,4,384,1024]{3,2,1,0:T(8,128)(2,1)}), bf16[1,4,96,1024]{3,2,1,0:T(8,128)(2,1)}) %reduce-scatter.15.cloned.1.call-update) | async-done | bytes 786448 | tf_op jit(solution)/shard_map/reduce_scatter | solution.py:49
  563.2 30.2 %reduce-scatter.13.cloned.1.call-done = bf16[1,4,96,1024]{3,2,1,0:T(8,128)(2,1)} async-done(((bf16[1,4,384,1024]{3,2,1,0:T(8,128)(2,1)}), bf16[1,4,96,1024]{3,2,1,0:T(8,128)(2,1)}) %reduce-scatter.13.cloned.1.call-update) | async-done | bytes 786448 | tf_op jit(solution)/shard_map/reduce_scatter | solution.py:49
  678.5 10.9 fusion.133
  706.6 15.5 reduce-scatter.17.cloned.1.call-done
  729.9 13.7 fusion.28
  743.6 11.9 fusion.22
  755.5 104.6 %reduce-scatter.31.cloned.1.call-done = f32[32,2]{1,0:T(8,128)} async-done(((f32[1024,2]{1,0:T(8,128)}), f32[32,2]{1,0:T(8,128)}) %reduce-scatter.31.cloned.1.call-update) | async-done | bytes 272
  867.2 37.0 %all-reduce.2 = (f32[1024]{0:T(1024)S(1)}, f32[1024]{0:T(1024)S(1)}) all-reduce(f32[1024]{0:T(1024)S(1)} %get-tuple-element.14, f32[1024]{0:T(1024)S(1)} %get-tuple-element.12), channel_id=12, replica_groups=mesh['expert'=8,'cuts'=4] {'expert','cuts'}, use_global_device_ids=true, to_apply=%region_46.47.clone | all-reduce | flops 2048 | bytes 16384
  906.9 87.9 %reduce-scatter.29.cloned.1.call-done = f32[32,32]{1,0:T(8,128)} async-done(((f32[1024,32]{1,0:T(8,128)}), f32[32,32]{1,0:T(8,128)}) %reduce-scatter.29.cloned.1.call-update) | async-done | bytes 4112 | tf_op jit(solution)/shard_map/reduce_scatter | solution.py:265
  994.7 142.4 %reduce-scatter.23.cloned.1.call-done = f32[32,1024]{1,0:T(8,128)} async-done(((f32[1024,1024]{1,0:T(8,128)}), f32[32,1024]{1,0:T(8,128)}) %reduce-scatter.23.cloned.1.call-update) | async-done | bytes 131088 | tf_op jit(solution)/shard_map/reduce_scatter | solution.py:262
  1137.1 357.4 %reduce-scatter.27.cloned.1.call-done = f32[128,1024]{1,0:T(8,128)} async-done(((f32[4096,1024]{1,0:T(8,128)}), f32[128,1024]{1,0:T(8,128)}) %reduce-scatter.27.cloned.1.call-update) | async-done | bytes 524304 | tf_op jit(solution)/shard_map/reduce_scatter | solution.py:264
  1494.5 361.8 %reduce-scatter.25.cloned.1.call-done = f32[32,4096]{1,0:T(8,128)} async-done(((f32[1024,4096]{1,0:T(8,128)}), f32[32,4096]{1,0:T(8,128)}) %reduce-scatter.25.cloned.1.call-update) | async-done | bytes 524304 | tf_op jit(solution)/shard_map/reduce_scatter | solution.py:263
  1856.3 162.5 %reduce-scatter.21.cloned.1.call-done = f32[32,3072]{1,0:T(8,128)} async-done(((f32[1024,3072]{1,0:T(8,128)}), f32[32,3072]{1,0:T(8,128)}) %reduce-scatter.21.cloned.1.call-update) | async-done | bytes 393232 | tf_op jit(solution)/shard_map/reduce_scatter | solution.py:261
  (337 shorter events, 265.0 us)
Async XLA Ops:
  7.2 75.4 %all-gather.11.cloned.1.call-start = ((), (), s32[]{:S(2)}) async-start(), calls=%async_computation.14 | async-start | bytes 7864320 | tf_op jit(solution)/shard_map/all_gather | solution.py:80
  7.9 116.1 %all-gather.15.cloned.1.call-start = ((), (), s32[]{:S(2)}) async-start(), calls=%async_computation.16 | async-start | bytes 2621440 | tf_op jit(solution)/shard_map/all_gather | solution.py:107
  88.6 73.0 %all-gather.13.cloned.1.call-start = ((), (), s32[]{:S(2)}) async-start(), calls=%async_computation.15 | async-start | bytes 2621440 | tf_op jit(solution)/shard_map/all_gather | solution.py:108
  89.4 109.2 %all-gather.17.cloned.1.call-start = ((), (), s32[]{:S(2)}) async-start(), calls=%async_computation.17 | async-start | bytes 2621440 | tf_op jit(solution)/shard_map/all_gather | solution.py:81
  90.0 190.6 %all-gather.23.cloned.1.call-start = ((), (), s32[]{:S(2)}) async-start(), calls=%async_computation.20 | async-start | bytes 3932160 | tf_op jit(solution)/shard_map/all_gather | solution.py:45
  90.1 536.1 %copy-start.47 = (f32[384]{0:T(512)}, f32[384]{0:T(512)S(1)}, u32[]{:S(2)}) copy-start(f32[384]{0:T(512)S(1)} %iota_convert_fusion) | copy-start | bytes 4612
  231.6 89.4 %all-gather.25.cloned.1.call-start = ((), (), s32[]{:S(2)}) async-start(), calls=%async_computation.22 | async-start | bytes 3932160 | tf_op jit(solution)/shard_map/all_gather | solution.py:45
  248.7 382.0 %copy-start.42 = (f32[256]{0:T(256)}, f32[256]{0:T(256)S(1)}, u32[]{:S(2)}) copy-start(f32[256]{0:T(256)S(1)} %get-tuple-element.48) | copy-start | bytes 3076
  248.8 305.1 %copy-start.56 = (f32[256]{0:T(256)}, f32[256]{0:T(256)S(1)}, u32[]{:S(2)}) copy-start(f32[256]{0:T(256)S(1)} %fusion.165) | copy-start | bytes 3076
  279.0 131.3 %all-gather.19.cloned.1.call-start = ((), (), s32[]{:S(2)}) async-start(), calls=%async_computation.18 | async-start | bytes 10485760 | tf_op jit(solution)/shard_map/all_gather | solution.py:82
  279.8 219.9 %all-gather.21.cloned.1.call-start = ((), (), s32[]{:S(2)}) async-start(), calls=%async_computation.19 | async-start | bytes 10485760 | tf_op jit(solution)/shard_map/all_gather | solution.py:83
  280.5 266.1 %reduce-scatter.15.cloned.1.call-start = ((), (), s32[]{:S(2)}) async-start(), calls=%async_computation.23 | async-start | bytes 3932160 | tf_op jit(solution)/shard_map/reduce_scatter | solution.py:49
  344.4 249.0 %reduce-scatter.13.cloned.1.call-start = ((), (), s32[]{:S(2)}) async-start(), calls=%async_computation.21 | async-start | bytes 3932160 | tf_op jit(solution)/shard_map/reduce_scatter | solution.py:49
  355.2 144.5 %copy-start.74 = (f32[256,1]{0,1:T(1,128)S(1)}, f32[256,1]{0,1:T(1,128)}, u32[]{:S(2)}) copy-start(f32[256,1]{0,1:T(1,128)} %get-tuple-element.34) | copy-start | bytes 3076
  549.2 46.8 %all-to-all-start.3 = ((bf16[1,4,96,1024]{3,1,0,2:T(4,128)(2,1)}), bf16[1,4,96,1024]{3,1,0,2:T(4,128)(2,1)S(1)}, u32[]{:S(2)}, u32[]{:S(2)}) async-start(bf16[1,4,96,1024]{3,1,0,2:T(4,128)(2,1)} %copy.69), calls=%async_computation.5 | async-start | bytes 1572864 | tf_op jit(solution)/shard_map/all_to_all | solution.py:52
  596.0 25.7 %all-to-all-start.1 = ((bf16[1,4,96,1024]{3,1,0,2:T(4,128)(2,1)}), bf16[1,4,96,1024]{3,1,0,2:T(4,128)(2,1)}, u32[]{:S(2)}, u32[]{:S(2)}) async-start(bf16[1,4,96,1024]{3,1,0,2:T(4,128)(2,1)} %copy.65), calls=%async_computation.2 | async-start | bytes 1572864 | tf_op jit(solution)/shard_map/all_to_all | solution.py:52
  600.6 106.0 %reduce-scatter.19.cloned.1.call-start = ((), (), s32[]{:S(2)}) async-start(), calls=%async_computation.25 | async-start | bytes 2621440 | tf_op jit(solution)/shard_map/reduce_scatter | solution.py:249
  650.2 71.9 %reduce-scatter.17.cloned.1.call-start = ((), (), s32[]{:S(2)}) async-start(), calls=%async_computation.24 | async-start | bytes 2621440 | tf_op jit(solution)/shard_map/reduce_scatter | solution.py:246
  672.3 187.7 %reduce-scatter.31.cloned.1.call-start = ((), (), s32[]{:S(2)}) async-start(), calls=%async_computation.31 | async-start | bytes 540672
  673.5 321.2 %reduce-scatter.29.cloned.1.call-start = ((), (), s32[]{:S(2)}) async-start(), calls=%async_computation.30 | async-start | bytes 540672 | tf_op jit(solution)/shard_map/reduce_scatter | solution.py:265
  674.8 462.3 %reduce-scatter.23.cloned.1.call-start = ((), (), s32[]{:S(2)}) async-start(), calls=%async_computation.27 | async-start | bytes 4325376 | tf_op jit(solution)/shard_map/reduce_scatter | solution.py:262
  677.5 817.0 %reduce-scatter.27.cloned.1.call-start = ((), (), s32[]{:S(2)}) async-start(), calls=%async_computation.29 | async-start | bytes 17301504 | tf_op jit(solution)/shard_map/reduce_scatter | solution.py:264
  689.4 1166.8 %reduce-scatter.25.cloned.1.call-start = ((), (), s32[]{:S(2)}) async-start(), calls=%async_computation.28 | async-start | bytes 17301504 | tf_op jit(solution)/shard_map/reduce_scatter | solution.py:263
  699.2 1319.5 %reduce-scatter.21.cloned.1.call-start = ((), (), s32[]{:S(2)}) async-start(), calls=%async_computation.26 | async-start | bytes 12976128 | tf_op jit(solution)/shard_map/reduce_scatter | solution.py:261
  (79 other events, 1191.8 us)
Sparse Core Ops, SparseCore 0:
  9.8 72.7 all-gather.10
  88.8 35.1 all-gather.14
  126.4 35.1 all-gather.12
  163.3 35.1 all-gather.16
  231.7 42.1 all-gather.22
  279.2 41.7 all-gather.24
  322.8 87.4 all-gather.18
  412.2 87.4 all-gather.20
  502.7 43.8 reduce-scatter.14
  549.4 43.8 reduce-scatter.12
  650.3 33.1 reduce-scatter.18
  686.9 35.1 reduce-scatter.16
  724.3 135.6 reduce-scatter.30
  862.7 131.9 reduce-scatter.28
  997.4 139.6 reduce-scatter.22
  1139.8 354.6 reduce-scatter.26
  1497.2 359.0 reduce-scatter.24
  1862.7 155.9 reduce-scatter.20
where the time goes:
time: 2040 us; the launch traced here: 2030 us
  waiting for transfers between devices  1610 us (79%)
  matrix products  192 us (9%)
  blocking collectives  120 us (6%)
  local copies, waits for them, and re-layouts  49.2 us (2%)
  other arithmetic  26.6 us (1%)
    reduce_scatter x1, waiting for transfers between devices, shards(): lax.psum_scatter(g_in, ('expert', 'cuts'), scatter_dimension=0, tiled=True)  362 us
    reduce_scatter x1, waiting for transfers between devices, shards(): lax.psum_scatter(g_out, ('expert', 'cuts'), scatter_dimension=0, tiled=True)  357 us
    reduce_scatter x1, waiting for transfers between devices, shards(): lax.psum_scatter(g_qkv, ('expert', 'cuts'), scatter_dimension=0, tiled=True)  162 us
    reduce_scatter x1, waiting for transfers between devices, shards(): lax.psum_scatter(g_attn_out, ('expert', 'cuts'), scatter_dimension=0, til...  142 us
    unnamed x19, waiting for transfers between devices  108 us
    reduce_scatter x1, waiting for transfers between devices, shards(): lax.psum_scatter(g_router, ('expert', 'cuts'), scatter_dimension=0, tiled...  87.9 us
    all_gather x1, waiting for transfers between devices, shards(): lax.all_gather(w_out, 'cuts', axis=0, tiled=True)  81.7 us
    reduce_scatter x2, waiting for transfers between devices, to_sources(): lax.psum_scatter(partial_rows[None].astype(jnp.bfloat16), 'cuts', scatter...  64.7 us
  transfers between devices with their start and end apart: 20, of which 17 were waited for; matrix products, arithmetic and copies ran while one was open for 10% of the time, Pallas kernels for 0%

commit v1 on v0

v1 whole, which is shorter than its diff:
```python
import jax
import jax.numpy as jnp
from jax import lax
from jax.sharding import PartitionSpec as P

HD = 64
BF = jnp.bfloat16
F32 = jnp.float32


def norm_parts(values):
    center = values - jnp.mean(values, axis=-1, keepdims=True)
    spread = jnp.mean(center * center, axis=-1, keepdims=True)
    inv = lax.rsqrt(spread + 1e-05)
    return center * inv, inv


def norm_back(grad, xhat, inv, gain):
    q = grad * gain
    mean_q = jnp.mean(q, axis=-1, keepdims=True)
    mean_qx = jnp.mean(q * xhat, axis=-1, keepdims=True)
    return (q - mean_q - xhat * mean_qx) * inv, jnp.sum(grad * xhat, axis=0)


def mm(left, right):
    return jnp.dot(left, right, preferred_element_type=F32)


def mm_nt(left, right):
    return lax.dot_general(left, right, (((1,), (1,)), ((), ())), preferred_element_type=F32)


def mm_tn(left, right):
    return lax.dot_general(left, right, (((0,), (0,)), ((), ())), preferred_element_type=F32)


def softmax_rows(logits):
    shifted = logits - jnp.max(logits, axis=-1, keepdims=True)
    row_exp = jnp.exp(shifted)
    return row_exp / jnp.sum(row_exp, axis=-1, keepdims=True)


def gather_cuts(rows):
    return lax.all_gather(rows, "cuts", axis=0, tiled=True)


def scatter_cuts(rows):
    return lax.psum_scatter(rows.astype(BF), "cuts", scatter_dimension=0, tiled=True)


def columns_to_cuts(rows):
    return lax.all_to_all(rows, "cuts", split_axis=1, concat_axis=0, tiled=True)


def rows_to_cuts(rows):
    return lax.all_to_all(rows, "cuts", split_axis=0, concat_axis=1, tiled=True)


def shards(
    block_input,
    routes,
    kept_mask,
    w_qkv,
    w_attn_out,
    w_in,
    w_out,
    w_router,
    w_mix,
    gain_attn,
    gain_ffn,
    expert_in,
    expert_out,
    cotangent,
):
    tokens, features = block_input.shape
    n_cuts = lax.axis_size("cuts")
    n_expert = lax.axis_size("expert")
    seq_len = tokens * n_cuts
    scaling = HD ** (-0.5)
    own = features // n_cuts
    heads = own // HD
    experts_all = w_router.shape[1]
    experts_here = expert_in.shape[0]
    capacity = 3 * tokens // (2 * experts_all)

    gains = gather_cuts(jnp.stack([gain_attn, gain_ffn], axis=1)).astype(F32)
    gain_one, gain_two = gains[:, 0], gains[:, 1]
    inputs = block_input.astype(F32)
    xhat_one, inv_one = norm_parts(inputs)
    normed = gather_cuts((xhat_one * gain_one).astype(BF))
    qkv_here = lax.all_to_all(
        w_qkv.reshape(own, 3, n_cuts, own), "cuts", split_axis=2, concat_axis=0, tiled=True
    ).reshape(features, 3 * own)
    joined = mm(normed, qkv_here).astype(BF)
    split = joined.reshape(seq_len, 3, heads, HD)
    q_heads, k_heads, v_heads = split[:, 0], split[:, 1], split[:, 2]
    spots = jnp.arange(seq_len, dtype=jnp.int32)
    visible = (spots[None, :] <= spots[:, None])[None]

    def masked_scores():
        scores = jnp.einsum("qhd,khd->hqk", q_heads, k_heads, preferred_element_type=F32) * scaling
        return jnp.where(visible, scores, -1e30)

    scores = masked_scores()
    peak = jnp.max(scores, axis=-1, keepdims=True)
    row_exp = jnp.exp(scores - peak)
    total = jnp.sum(row_exp, axis=-1, keepdims=True)
    weights_p = (row_exp / total).astype(BF)
    heads_here = jnp.einsum("hqk,khd->qhd", weights_p, v_heads, preferred_element_type=F32)
    log_norm = peak + jnp.log(total)
    head_out = rows_to_cuts(heads_here.reshape(seq_len, own).astype(BF))
    attn_full = gather_cuts(w_attn_out)
    small_full = gather_cuts(jnp.concatenate([w_router, w_mix], axis=1))
    hidden = inputs + mm(head_out, attn_full)
    xhat_two, inv_two = norm_parts(hidden)
    second = (xhat_two * gain_two).astype(BF)

    logits = mm(second, small_full)
    onehot = (routes[:, None] == jnp.arange(experts_all, dtype=jnp.int32)[None, :]).astype(F32)
    router_p = softmax_rows(logits[:, :experts_all])
    mixing = softmax_rows(logits[:, experts_all:])
    gate = jnp.sum(router_p * onehot, axis=1)
    grad = cotangent.astype(F32)
    d_dense = (grad * mixing[:, 0:1]).astype(BF)
    d_moe = grad * mixing[:, 1:2]
    d_picked = (d_moe * gate[:, None]).astype(BF)

    onehot_kept = onehot * kept_mask.astype(F32)[:, None]
    lower_tri = (jnp.arange(tokens)[:, None] >= jnp.arange(tokens)[None, :]).astype(BF)
    running = mm(lower_tri, onehot_kept.astype(BF))
    slot_num = jnp.sum(onehot_kept * running, axis=1) - 1.0
    target = routes.astype(F32) * capacity + slot_num
    columns = jnp.arange(experts_all * capacity, dtype=jnp.int32).astype(F32)
    placer = ((columns[None, :] == target[:, None]) & (kept_mask[:, None] > 0)).astype(BF)
    both = jnp.concatenate([second, d_picked], axis=1)
    slots = mm_tn(placer, both).astype(BF)
    grid = slots.reshape(n_expert, experts_here, capacity, 2 * features)
    moved = lax.all_to_all(grid, "expert", split_axis=0, concat_axis=2, tiled=True)
    rows_both = lax.all_gather(moved, "cuts", axis=2, tiled=True)[0]
    rows_in, d_rows = rows_both[:, :, :features], rows_both[:, :, features:]

    ffn_both = gather_cuts(jnp.concatenate([second, d_dense], axis=1))
    second_all, d_dense_all = ffn_both[:, :features], ffn_both[:, features:]
    in_here = columns_to_cuts(w_in)
    up_proj = mm(second_all, in_here)
    activ, gelu_pull = jax.vjp(jax.nn.gelu, up_proj)
    activ_low = activ.astype(BF)
    dense_part = mm(activ_low, w_out)
    d_activ = mm_nt(d_dense_all, w_out)
    g_out = mm_tn(activ_low, d_dense_all)
    d_up = gelu_pull(d_activ)[0].astype(BF)
    g_in = mm_tn(second_all, d_up)
    d_second_part = mm_nt(d_up, in_here)
    ffn_sums = scatter_cuts(jnp.concatenate([dense_part, d_second_part], axis=1))
    dense, d_second_ffn = ffn_sums[:, :features].astype(F32), ffn_sums[:, features:].astype(F32)

    first = jnp.einsum("erd,edh->erh", rows_in, expert_in, preferred_element_type=F32)
    expert_act, expert_pull = jax.vjp(jax.nn.gelu, first)
    expert_low = expert_act.astype(BF)
    partial_out = jnp.einsum("erh,ehd->erd", expert_low, expert_out, preferred_element_type=F32)
    d_expert_act = jnp.einsum("erd,ehd->erh", d_rows, expert_out, preferred_element_type=F32)
    d_first = expert_pull(d_expert_act)[0].astype(BF)
    d_rows_in = jnp.einsum("erh,edh->erd", d_first, expert_in, preferred_element_type=F32)
    g_expert_out = jnp.einsum("erh,erd->ehd", expert_low, d_rows, preferred_element_type=F32)
    g_expert_in = jnp.einsum("erd,erh->edh", rows_in, d_first, preferred_element_type=F32)
    back = jnp.concatenate([partial_out, d_rows_in], axis=2).astype(BF)
    summed = lax.psum_scatter(back[None], "cuts", scatter_dimension=2, tiled=True)
    returned = lax.all_to_all(summed, "expert", split_axis=2, concat_axis=0, tiled=True)
    picked_both = mm(placer, returned.reshape(-1, 2 * features))
    picked, d_picked_in = picked_both[:, :features], picked_both[:, features:]

    moe_val = gate[:, None] * picked
    block_out = (hidden + mixing[:, 0:1] * dense + mixing[:, 1:2] * moe_val).astype(BF)
    d_mixing = jnp.stack([jnp.sum(grad * dense, axis=1), jnp.sum(grad * moe_val, axis=1)], axis=1)
    d_gate = jnp.sum(d_moe * picked, axis=1)
    d_router = router_p * (onehot - gate[:, None]) * d_gate[:, None]
    d_mix = mixing * (d_mixing - jnp.sum(mixing * d_mixing, axis=1, keepdims=True))
    d_small = jnp.concatenate([d_router, d_mix], axis=1).astype(BF)
    g_small = mm_tn(second, d_small)
    d_second = d_second_ffn + mm_nt(d_small, small_full) + d_picked_in
    d_hidden_norm, g_gain_two = norm_back(d_second, xhat_two, inv_two, gain_two)
    d_hidden = grad + d_hidden_norm
    d_attn = d_hidden.astype(BF)
    g_attn_out = mm_tn(head_out, d_attn)
    d_heads = columns_to_cuts(mm_nt(d_attn, attn_full).astype(BF)).reshape(seq_len, heads, HD)

    soft_p = jnp.exp(masked_scores() - log_norm)
    d_soft = jnp.einsum("qhd,khd->hqk", d_heads, v_heads, preferred_element_type=F32)
    delta = jnp.sum(soft_p * d_soft, axis=-1, keepdims=True)
    d_scores = (soft_p * (d_soft - delta)).astype(BF)
    d_query = jnp.einsum("hqk,khd->qhd", d_scores, k_heads, preferred_element_type=F32) * scaling
    d_keys = jnp.einsum("hqk,qhd->khd", d_scores, q_heads, preferred_element_type=F32) * scaling
    d_values = jnp.einsum("hqk,qhd->khd", soft_p.astype(BF), d_heads, preferred_element_type=F32)
    d_joined = jnp.stack([d_query, d_keys, d_values], axis=1).reshape(seq_len, 3 * own).astype(BF)
    g_qkv = mm_tn(normed, d_joined)
    d_normed = scatter_cuts(mm_nt(d_joined, qkv_here)).astype(F32)
    d_input_norm, g_gain_one = norm_back(d_normed, xhat_one, inv_one, gain_one)
    d_block_input = d_hidden + d_input_norm

    def over_experts(part):
        return lax.psum_scatter(part.astype(BF), "expert", scatter_dimension=0, tiled=True)

    s_in = rows_to_cuts(over_experts(g_in)).astype(F32)
    s_out = over_experts(g_out)
    swap = [
        ((flat % n_expert) * n_cuts + flat // n_expert, flat) for flat in range(n_expert * n_cuts)
    ]
    s_out = lax.ppermute(s_out, ("expert", "cuts"), swap).astype(F32)
    s_qkv = over_experts(g_qkv)
    deep = s_qkv.shape[0]
    s_qkv = lax.all_to_all(
        s_qkv.reshape(deep, 3, 1, own), "cuts", split_axis=0, concat_axis=2, tiled=True
    )
    s_qkv = s_qkv.reshape(-1, 3 * features).astype(F32)
    s_attn_out = lax.psum_scatter(
        g_attn_out.astype(BF), ("expert", "cuts"), scatter_dimension=0, tiled=True
    ).astype(F32)
    tiny = jnp.concatenate([g_small, g_gain_one[:, None], g_gain_two[:, None]], axis=1)
    s_tiny = lax.psum_scatter(tiny, ("expert", "cuts"), scatter_dimension=0, tiled=True)
    return (
        block_out,
        d_block_input,
        s_qkv,
        s_attn_out,
        s_in,
        s_out,
        s_tiny[:, :experts_all],
        s_tiny[:, experts_all : experts_all + 2],
        s_tiny[:, experts_all + 2],
        s_tiny[:, experts_all + 3],
        g_expert_in,
        g_expert_out,
    )


def solution(mesh):
    both = ("expert", "cuts")
    placed = (
        P(both, None),
        P(both),
        P(both),
        P("cuts", None),
        P("cuts", None),
        P("cuts", None),
        P("cuts", None),
        P("cuts", None),
        P("cuts", None),
        P("cuts"),
        P("cuts"),
        P("expert", None, "cuts"),
        P("expert", "cuts", None),
        P(both, None),
    )
    results = (
        P(both, None),
        P(both, None),
        P(both, None),
        P(both, None),
        P(both, None),
        P(both, None),
        P(both, None),
        P(both, None),
        P(both),
        P(both),
        P("expert", None, "cuts"),
        P("expert", "cuts", None),
    )
    return jax.shard_map(
        shards, mesh=mesh, in_specs=placed, out_specs=results, check_vma=False
    )
```

time: 2040 us -> 897 us (0.44)
  waiting for transfers between devices: 1610 us -> 455 us
  matrix products: 192 us -> 159 us
  starting transfers between devices: 10.3 us -> 41.2 us
  other arithmetic: 26.6 us -> 49.7 us
    reduce_scatter x9 -> x7, waiting for transfers between devices: 1190 us -> 182 us  [the longest x1 114 us: shards(): lax.psum_scatter(g_attn_out.astype(BF), ('expert', 'cuts'), scatter_dimen...]
    all_gather x8 -> x4, waiting for transfers between devices: 303 us -> 76.9 us  [the longest x1 65.3 us: shards(): rows_both = lax.all_gather(moved, 'cuts', axis=2, tiled=True)[0]]
    all_to_all x2 -> x6, waiting for transfers between devices: 8.4 us -> 62.1 us  [the longest x1 30.9 us: shards(): lax.all_to_all(summed, 'expert', split_axis=2, concat_axis=0, tiled=True)]
    all_to_all x2, blocking collectives: 48.7 us -> 85.9 us  [the longest x1 43.7 us: columns_to_cuts(): return lax.all_to_all(rows, 'cuts', split_axis=1, concat_axis=0, tiled=True)]
    unnamed x1 -> x0, blocking collectives: 37 us -> none
    dot_general x51 -> x29, matrix products: 181 us -> 149 us  [the longest x6 22.3 us: mm_tn(): lax.dot_general(left, right, (((0,), (0,)), ((), ())), preferred_element_...]
    all_to_all x2 -> x6, starting transfers between devices: 9.22 us -> 38.6 us  [the longest x1 19 us: shards(): lax.all_to_all(s_qkv.reshape(deep, 3, 1, own), 'cuts', split_axis=0, conc...]
    unnamed x19 -> x13, waiting for transfers between devices: 108 us -> 134 us
  transfers between devices with their start and end apart: 20 -> 19, of which waited for: 17 -> 14; matrix products, arithmetic and copies ran while one was open for 10% -> 26% of each run, Pallas kernels for 0% -> 0%
where the time goes in v1:
time: 897 us; the launch traced here: 885 us
  waiting for transfers between devices  455 us (51%)
  matrix products  159 us (18%)
  blocking collectives  109 us (12%)
  local copies, waits for them, and re-layouts  55.3 us (6%)
  other arithmetic  49.7 us (6%)
  starting transfers between devices  41.2 us (5%)
  between operations  15.2 us (2%)
    unnamed x13, waiting for transfers between devices  134 us
    reduce_scatter x1, waiting for transfers between devices, shards(): lax.psum_scatter(g_attn_out.astype(BF), ('expert', 'cuts'), scatter_dimen...  114 us
    all_gather x1, waiting for transfers between devices, shards(): rows_both = lax.all_gather(moved, 'cuts', axis=2, tiled=True)[0]  65.3 us
    all_to_all x1, blocking collectives, columns_to_cuts(): return lax.all_to_all(rows, 'cuts', split_axis=1, concat_axis=0, tiled=True)  43.7 us
    all_to_all x1, blocking collectives, shards(): lax.all_to_all(grid, 'expert', split_axis=0, concat_axis=2, tiled=True)  42.2 us
    reduce_scatter x2, waiting for transfers between devices, scatter_cuts(): lax.psum_scatter(rows.astype(BF), 'cuts', scatter_dimension=0, tiled=True)  35 us
    all_to_all x1, waiting for transfers between devices, shards(): lax.all_to_all(summed, 'expert', split_axis=2, concat_axis=0, tiled=True)  30.9 us
    reduce_scatter x1, waiting for transfers between devices, shards(): lax.psum_scatter(back[None], 'cuts', scatter_dimension=2, tiled=True)  24.8 us
  transfers between devices with their start and end apart: 19, of which 14 were waited for; matrix products, arithmetic and copies ran while one was open for 26% of the time, Pallas kernels for 0%

profile of v1, /device:TPU:0, one launch (start us, length us, event | category | flops | bytes accessed | tf_op | source)
XLA Modules:
  0.0 884.8 jit_solution(11240643413471796016)
XLA Ops:
  11.3 9.6 %all_gather.18 = bf16[1024,2]{0,1:T(2,128)(2,1)S(1)} all-gather(bf16[256,2]{0,1:T(2,128)(2,1)S(1)} %pad_maximum_fusion.11), channel_id=1, replica_groups=mesh['expert'=8,'cuts'=4] {'cuts'}, dimensions={0}, use_global_device_ids=true | all-gather | bytes 5120 | tf_op jit(solution)/shard_map/all_gather | solution.py:44
  34.4 22.0 %all-to-all-done = bf16[256,3,4,256]{0,3,1,2:T(8,128)(2,1)} async-done(((bf16[256,3,4,256]{0,3,1,2:T(8,128)(2,1)}), bf16[256,3,4,256]{0,3,1,2:T(8,128)(2,1)}, u32[]{:S(2)}, u32[]{:S(2)}) %all-to-all-start) | async-done | bytes 1572896 | tf_op jit(solution)/shard_map/all_to_all | solution.py:91
  60.5 11.6 %all-gather.5.cloned.1.call-done = bf16[1024,1024]{1,0:T(8,128)(2,1)} async-done(((bf16[256,1024]{1,0:T(8,128)(2,1)}), bf16[1024,1024]{1,0:T(8,128)(2,1)}) %all-gather.5.cloned.1.call-update) | async-done | bytes 2097168 | tf_op jit(solution)/shard_map/all_gather | solution.py:44
  75.9 7.8 fusion.96
  83.8 8.0 fusion
  91.8 7.8 fusion.54
  104.3 14.0 %all_gather.21 = bf16[1024,34]{0,1:T(8,128)(2,1)S(1)} all-gather(bf16[256,34]{0,1:T(8,128)(2,1)S(1)} %pad_maximum_fusion.6), channel_id=1, replica_groups=mesh['expert'=8,'cuts'=4] {'cuts'}, dimensions={0}, use_global_device_ids=true | all-gather | bytes 87040 | tf_op jit(solution)/shard_map/all_gather | solution.py:44
  133.4 42.2 %all_to_all.121 = bf16[8,4,12,2048]{3,1,2,0:T(4,128)(2,1)S(1)} all-to-all(bf16[8,4,12,2048]{3,1,2,0:T(4,128)(2,1)S(1)} %copy.134), channel_id=1, replica_groups=mesh['expert'=8,'cuts'=4] {'expert'}, dimensions={0} | all-to-all | bytes 3145728 | tf_op jit(solution)/shard_map/all_to_all | solution.py:138
  180.0 65.3 %all-gather.11.cloned.1.call-done = bf16[1,4,384,2048]{3,2,1,0:T(8,128)(2,1)} async-done(((bf16[1,4,96,2048]{3,2,1,0:T(8,128)(2,1)}), bf16[1,4,384,2048]{3,2,1,0:T(8,128)(2,1)}) %all-gather.11.cloned.1.call-update) | async-done | bytes 6291472 | tf_op jit(solution)/shard_map/all_gather | solution.py:139
  252.3 13.0 %fusion.12 = bf16[4,384,1024]{2,1,0:T(8,128)(2,1)} fusion(f32[4,384,1024]{2,1,0:T(8,128)S(1)} %fusion.28, bf16[4,1024,1024]{2,1,0:T(8,128)(2,1)} %param.26, bf16[4,384,2048]{2,1,0:T(8,128)(2,1)S(1)} %bitcast.139), kind=kOutput, calls=%fused_computation.19 | convolution fusion | flops 3252682752 | bytes 20971520 | tf_op jit(solution)/shard_map/erd,ehd->erh/dot_general | solution.py:161
  265.3 9.5 %convert_bitcast_fusion = bf16[1,4,384,1024]{3,2,1,0:T(8,128)(2,1)} fusion(bf16[4,384,1024]{2,1,0:T(8,128)(2,1)} %fusion.12, bf16[4,1024,1024]{2,1,0:T(8,128)(2,1)} %param.25), kind=kOutput, calls=%fused_computation.35 | convolution fusion | flops 3222798336 | bytes 14680064 | tf_op jit(solution)/shard_map/erh,edh->erd/dot_general | solution.py:163
  274.8 9.9 %convert_bitcast_fusion.1 = bf16[1,4,384,1024]{3,2,1,0:T(8,128)(2,1)} fusion(bf16[4,1024,1024]{2,1,0:T(8,128)(2,1)} %param.26, f32[4,384,1024]{2,1,0:T(8,128)S(1)} %fusion.28), kind=kOutput, calls=%fused_computation.36 | convolution fusion | flops 3236954112 | bytes 17825792 | tf_op jit(solution)/shard_map/erh,ehd->erd/dot_general | solution.py:160
  295.4 43.7 %all_to_all.122 = bf16[256,4,1024]{0,2,1:T(8,128)(2,1)} all-to-all(bf16[256,4,1024]{0,2,1:T(8,128)(2,1)} %bitcast.131), channel_id=1, replica_groups=mesh['expert'=8,'cuts'=4] {'cuts'}, dimensions={1} | all-to-all | bytes 4194304 | tf_op jit(solution)/shard_map/all_to_all | solution.py:52
  361.7 24.8 %reduce-scatter.13.cloned.1.call-done = bf16[1,4,96,2048]{3,2,1,0:T(8,128)(2,1)} async-done(((bf16[1,4,384,2048]{3,2,1,0:T(8,128)(2,1)}), bf16[1,4,96,2048]{3,2,1,0:T(8,128)(2,1)}) %reduce-scatter.13.cloned.1.call-update) | async-done | bytes 1572880 | tf_op jit(solution)/shard_map/reduce_scatter | solution.py:167
  401.8 30.9 %all-to-all-done.4 = bf16[1,4,96,2048]{3,1,0,2:T(4,128)(2,1)S(1)} async-done(((bf16[1,4,96,2048]{3,1,0,2:T(4,128)(2,1)}), bf16[1,4,96,2048]{3,1,0,2:T(4,128)(2,1)S(1)}, u32[]{:S(2)}, u32[]{:S(2)}) %all-to-all-start.4) | async-done | bytes 1572896 | tf_op jit(solution)/shard_map/all_to_all | solution.py:168
  461.0 11.3 %multiply_reduce_fusion = (f32[4,1024]{1,0:T(4,128)S(1)}, f32[4,1024,1024]{1,2,0:T(8,128)}) fusion(f32[4,1024,1024]{1,2,0:T(8,128)} %get-tuple-element.103, f32[4,1024]{1,0:T(4,128)S(1)} %log_add_fusion, bf16[1024,4,64]{0,2,1:T(8,128)(2,1)S(1)} %reshape.197, bf16[1024,3,4,64]{0,3,2,1:T(8,128)(2,1)} %bitcast.148), kind=kOutput, calls=%fused_computation.1 | convolution fusion | flops 549449728 | bytes 34635776 | tf_op jit(solution)/shard_map/qhd,khd->hqk/dot_general | solution.py:188
  472.3 12.2 %multiply_convert_fusion = bf16[4,1024,1024]{1,2,0:T(8,128)(2,1)S(1)} fusion(f32[4,1024,1024]{1,2,0:T(8,128)} %get-tuple-element.108, f32[4,1024,1024]{1,2,0:T(8,128)} %get-tuple-element.103, f32[4,1024]{1,0:T(4,128)S(1)} %get-tuple-element.107, f32[4,1024]{1,0:T(4,128)S(1)} %log_add_fusion), kind=kLoop, calls=%fused_computation | loop fusion | flops 16777216 | bytes 41975808 | tf_op jit(solution)/shard_map/convert_element_type | solution.py:190
  523.8 13.6 %fusion.26 = f32[4,1024,1024]{2,1,0:T(8,128)} fusion(bf16[4,384,1024]{2,1,0:T(8,128)(2,1)} %fusion.12, bf16[4,384,2048]{2,1,0:T(8,128)(2,1)} %bitcast.137), kind=kOutput, calls=%fused_computation.42 | convolution fusion | flops 3221225472 | bytes 23068672 | tf_op jit(solution)/shard_map/erd,erh->edh/dot_general | solution.py:165
  537.4 14.9 %fusion.20 = f32[4,1024,1024]{2,1,0:T(8,128)} fusion(bf16[4,384,2048]{2,1,0:T(8,128)(2,1)} %bitcast.138, f32[4,384,1024]{2,1,0:T(8,128)} %copy-done.10), kind=kOutput, calls=%fused_computation.38 | convolution fusion | flops 3235381248 | bytes 26214400 | tf_op jit(solution)/shard_map/erh,erd->ehd/dot_general | solution.py:164
  552.3 7.5 reduce-scatter.17.cloned.1.call-done
  561.7 19.0 %all-to-all-start.6 = ((bf16[128,3,1,256]{3,1,2,0:T(4,128)(2,1)}), bf16[128,3,1,256]{3,1,2,0:T(4,128)(2,1)S(1)}, u32[]{:S(2)}, u32[]{:S(2)}) async-start(bf16[128,3,1,256]{3,1,2,0:T(4,128)(2,1)} %copy.144), calls=%async_computation.10 | async-start | bytes 524288 | tf_op jit(solution)/shard_map/all_to_all | solution.py:211
  587.5 113.9 %reduce-scatter.19.cloned.1.call-done = bf16[32,1024]{1,0:T(8,128)(2,1)} async-done(((bf16[1024,1024]{1,0:T(8,128)(2,1)}), bf16[32,1024]{1,0:T(8,128)(2,1)}) %reduce-scatter.19.cloned.1.call-update) | async-done | bytes 65552 | tf_op jit(solution)/shard_map/reduce_scatter | solution.py:215
  702.9 32.7 %reduce-scatter.15.cloned.1.call-done = bf16[256,1024]{1,0:T(8,128)(2,1)} async-done(((bf16[1024,1024]{1,0:T(8,128)(2,1)}), bf16[256,1024]{1,0:T(8,128)(2,1)}) %reduce-scatter.15.cloned.1.call-update) | async-done | bytes 524304 | tf_op jit(solution)/shard_map/reduce_scatter | solution.py:48
  741.0 133.2 %reduce-scatter.25.cloned.1.call-done = f32[32,36]{1,0:T(8,128)} async-done(((f32[1024,36]{1,0:T(8,128)}), f32[32,36]{1,0:T(8,128)}) %reduce-scatter.25.cloned.1.call-update) | async-done | bytes 4624
  (209 shorter events, 191.3 us)
Async XLA Ops:
  7.2 340.8 %copy-start = (bf16[1024,1024]{1,0:T(8,128)(2,1)S(1)}, bf16[1024,1024]{1,0:T(8,128)(2,1)}, u32[]{:S(2)}) copy-start(bf16[1024,1024]{1,0:T(8,128)(2,1)} %param.20) | copy-start | bytes 6291460
  7.2 64.9 %all-gather.5.cloned.1.call-start = ((), (), s32[]{:S(2)}) async-start(), calls=%async_computation.16 | async-start | bytes 2621440 | tf_op jit(solution)/shard_map/all_gather | solution.py:44
  28.9 27.5 %all-to-all-start = ((bf16[256,3,4,256]{0,3,1,2:T(8,128)(2,1)}), bf16[256,3,4,256]{0,3,1,2:T(8,128)(2,1)}, u32[]{:S(2)}, u32[]{:S(2)}) async-start(bf16[256,3,4,256]{0,3,1,2:T(8,128)(2,1)} %copy.126), calls=%async_computation | async-start | bytes 3145728 | tf_op jit(solution)/shard_map/all_to_all | solution.py:91
  33.3 85.3 %all-gather.7.cloned.1.call-start = ((), (), s32[]{:S(2)}) async-start(), calls=%async_computation.17 | async-start | bytes 2621440 | tf_op jit(solution)/shard_map/all_gather | solution.py:44
  100.8 17.8 %all-to-all-start.1 = ((bf16[4,256,256]{1,2,0:T(8,128)(2,1)}), bf16[4,256,256]{1,2,0:T(8,128)(2,1)S(1)}, u32[]{:S(2)}, u32[]{:S(2)}) async-start(bf16[4,256,256]{1,2,0:T(8,128)(2,1)} %copy.129), calls=%async_computation.1 | async-start | bytes 1048576 | tf_op jit(solution)/shard_map/all_to_all | solution.py:56
  104.3 141.1 %all-gather.11.cloned.1.call-start = ((), (), s32[]{:S(2)}) async-start(), calls=%async_computation.20 | async-start | bytes 7864320 | tf_op jit(solution)/shard_map/all_gather | solution.py:139
  177.6 165.5 %all-gather.9.cloned.1.call-start = ((), (), s32[]{:S(2)}) async-start(), calls=%async_computation.18 | async-start | bytes 5242880 | tf_op jit(solution)/shard_map/all_gather | solution.py:44
  180.0 206.6 %reduce-scatter.13.cloned.1.call-start = ((), (), s32[]{:S(2)}) async-start(), calls=%async_computation.21 | async-start | bytes 7864320 | tf_op jit(solution)/shard_map/reduce_scatter | solution.py:167
  291.3 150.7 %reduce-scatter.11.cloned.1.call-start = ((), (), s32[]{:S(2)}) async-start(), calls=%async_computation.19 | async-start | bytes 5242880 | tf_op jit(solution)/shard_map/reduce_scatter | solution.py:48
  390.3 42.4 %all-to-all-start.4 = ((bf16[1,4,96,2048]{3,1,0,2:T(4,128)(2,1)}), bf16[1,4,96,2048]{3,1,0,2:T(4,128)(2,1)S(1)}, u32[]{:S(2)}, u32[]{:S(2)}) async-start(bf16[1,4,96,2048]{3,1,0,2:T(4,128)(2,1)} %copy.136), calls=%async_computation.6 | async-start | bytes 3145728 | tf_op jit(solution)/shard_map/all_to_all | solution.py:168
  394.9 118.1 %reduce-scatter.21.cloned.1.call-start = ((), (), s32[]{:S(2)}) async-start(), calls=%async_computation.25 | async-start | bytes 2359296 | tf_op jit(solution)/shard_map/reduce_scatter | solution.py:201
  448.8 11.6 %all-to-all-start.5 = ((bf16[256,4,256]{2,0,1:T(8,128)(2,1)}), bf16[256,4,256]{2,0,1:T(8,128)(2,1)S(1)}, u32[]{:S(2)}, u32[]{:S(2)}) async-start(bf16[256,4,256]{2,0,1:T(8,128)(2,1)} %bitcast.126), calls=%async_computation.7 | async-start | bytes 1048576 | tf_op jit(solution)/shard_map/all_to_all | solution.py:52
  452.2 65.1 %reduce-scatter.23.cloned.1.call-start = ((), (), s32[]{:S(2)}) async-start(), calls=%async_computation.26 | async-start | bytes 2359296 | tf_op jit(solution)/shard_map/reduce_scatter | solution.py:201
  459.3 100.5 %reduce-scatter.17.cloned.1.call-start = ((), (), s32[]{:S(2)}) async-start(), calls=%async_computation.23 | async-start | bytes 1769472 | tf_op jit(solution)/shard_map/reduce_scatter | solution.py:201
  505.7 195.7 %reduce-scatter.19.cloned.1.call-start = ((), (), s32[]{:S(2)}) async-start(), calls=%async_computation.24 | async-start | bytes 2162688 | tf_op jit(solution)/shard_map/reduce_scatter | solution.py:215
  507.9 227.7 %reduce-scatter.15.cloned.1.call-start = ((), (), s32[]{:S(2)}) async-start(), calls=%async_computation.22 | async-start | bytes 2621440 | tf_op jit(solution)/shard_map/reduce_scatter | solution.py:48
  513.1 9.0 %all-to-all-start.7 = ((bf16[4,32,1024]{2,1,0:T(8,128)(2,1)}), bf16[4,32,1024]{2,1,0:T(8,128)(2,1)S(1)}, u32[]{:S(2)}, u32[]{:S(2)}) async-start(bf16[4,32,1024]{2,1,0:T(8,128)(2,1)} %bitcast.158), calls=%async_computation.13 | async-start | bytes 524288 | tf_op jit(solution)/shard_map/all_to_all | solution.py:56
  517.4 5.6 collective-permute-start
  552.2 183.4 %copy-start.19 = (f32[1024,1]{0,1:T(1,128)S(1)}, f32[1024,1]{0,1:T(1,128)}, u32[]{:S(2)}) copy-start(f32[1024,1]{0,1:T(1,128)} %copy-done.18) | copy-start | bytes 12292
  552.2 183.4 %copy-start.21 = (f32[256]{0:T(256)S(1)}, f32[256]{0:T(256)}, u32[]{:S(2)}) copy-start(f32[256]{0:T(256)} %copy-done.20) | copy-start | bytes 3076
  552.2 183.4 %copy-start.24 = (f32[256]{0:T(256)S(1)}, f32[256]{0:T(256)}, u32[]{:S(2)}) copy-start(f32[256]{0:T(256)} %copy-done.23) | copy-start | bytes 3076
  561.7 24.5 %all-to-all-start.6 = ((bf16[128,3,1,256]{3,1,2,0:T(4,128)(2,1)}), bf16[128,3,1,256]{3,1,2,0:T(4,128)(2,1)S(1)}, u32[]{:S(2)}, u32[]{:S(2)}) async-start(bf16[128,3,1,256]{3,1,2,0:T(4,128)(2,1)} %copy.144), calls=%async_computation.10 | async-start | bytes 524288 | tf_op jit(solution)/shard_map/all_to_all | solution.py:211
  580.8 293.5 %reduce-scatter.25.cloned.1.call-start = ((), (), s32[]{:S(2)}) async-start(), calls=%async_computation.27 | async-start | bytes 540672
  586.2 291.5 %copy-start.1 = (bf16[1024,1024]{1,0:T(8,128)(2,1)S(1)}, bf16[1024,1024]{1,0:T(8,128)(2,1)}, u32[]{:S(2)}) copy-start(bf16[1024,1024]{1,0:T(8,128)(2,1)} %param.20) | copy-start | bytes 6291460
  (30 other events, 545.1 us)
Sparse Core Ops, SparseCore 0:
  23.7 48.3 all-gather.4
  73.9 39.9 all-gather.6
  177.8 67.5 all-gather.10
  247.6 52.5 all-gather.8
  303.6 82.8 reduce-scatter.12
  389.4 52.5 reduce-scatter.10
  444.3 35.6 reduce-scatter.20
  482.3 35.0 reduce-scatter.22
  519.7 40.0 reduce-scatter.16
  561.9 139.4 reduce-scatter.18
  704.4 31.1 reduce-scatter.14
  738.4 135.7 reduce-scatter.24

commit v2 on v1

--- a/solution.py
+++ b/solution.py
@@ -1,11 +1,17 @@
+import functools
+import math
+
 import jax
 import jax.numpy as jnp
 from jax import lax
+from jax.experimental import pallas as pl
+from jax.experimental.pallas import tpu as pltpu
 from jax.sharding import PartitionSpec as P
 
 HD = 64
 BF = jnp.bfloat16
 F32 = jnp.float32
+MESH = pl.DeviceIdType.MESH
 
 
 def norm_parts(values):
@@ -54,6 +60,442 @@
 
 def rows_to_cuts(rows):
     return lax.all_to_all(rows, "cuts", split_axis=0, concat_axis=1, tiled=True)
+
+
+def ring_mod(index, count):
+    return lax.rem(index, count)
+
+
+def small_kernel(n_expert, n_cuts, src, out, by_expert, mine, by_cuts, send_a, recv_a, send_b, recv_b):
+    me, cut = lax.axis_index("expert"), lax.axis_index("cuts")
+    width = out.shape[1]
+    barrier = pltpu.get_barrier_semaphore()
+    for step in range(1, n_expert):
+        peer = ring_mod(me + step, n_expert)
+        pl.semaphore_signal(barrier, inc=1, device_id=(peer, cut), device_id_type=MESH)
+    for step in range(1, n_cuts):
+        peer = ring_mod(cut + step, n_cuts)
+        pl.semaphore_signal(barrier, inc=1, device_id=(me, peer), device_id_type=MESH)
+    pl.semaphore_wait(barrier, n_expert + n_cuts - 2)
+
+    def part(owner):
+        return src.at[:, pl.ds(pl.multiple_of(owner * width, 128), width)]
+
+    copies = []
+    for step in range(1, n_expert):
+        peer = ring_mod(me + step, n_expert)
+        copies.append(
+            pltpu.make_async_remote_copy(
+                src_ref=part(peer),
+                dst_ref=by_expert.at[step],
+                send_sem=send_a.at[step],
+                recv_sem=recv_a.at[step],
+                device_id=(peer, cut),
+                device_id_type=MESH,
+            )
+        )
+        copies[-1].start()
+    total = src[:, pl.ds(pl.multiple_of(me * width, 128), width)]
+    for step in range(1, n_expert):
+        copies[step - 1].wait()
+        total = total + by_expert[step]
+    mine[...] = total
+    copies = []
+    for step in range(1, n_cuts):
+        peer = ring_mod(cut + step, n_cuts)
+        copies.append(
+            pltpu.make_async_remote_copy(
+                src_ref=mine,
+                dst_ref=by_cuts.at[step],
+                send_sem=send_b.at[step],
+                recv_sem=recv_b.at[step],
+                device_id=(me, peer),
+                device_id_type=MESH,
+            )
+        )
+        copies[-1].start()
+    for step in range(1, n_cuts):
+        copies[step - 1].wait()
+        total = total + by_cuts[step]
+    out[...] = total
+
+
+def sum_small(values, n_expert, n_cuts):
+    rows, features = values.shape
+    width = features // n_expert
+    pad = -width % 128
+    if pad:
+        values = jnp.pad(values.reshape(rows, n_expert, width), ((0, 0), (0, 0), (0, pad)))
+        values = values.reshape(rows, n_expert * (width + pad))
+    wide = width + pad
+    summed = pl.pallas_call(
+        functools.partial(small_kernel, n_expert, n_cuts),
+        name="sum_small",
+        out_shape=jax.ShapeDtypeStruct((rows, wide), F32),
+        in_specs=[pl.BlockSpec(memory_space=pltpu.VMEM)],
+        out_specs=pl.BlockSpec(memory_space=pltpu.VMEM),
+        scratch_shapes=[
+            pltpu.VMEM((n_expert, rows, wide), F32),
+            pltpu.VMEM((rows, wide), F32),
+            pltpu.VMEM((n_cuts, rows, wide), F32),
+            pltpu.SemaphoreType.DMA((n_expert,)),
+            pltpu.SemaphoreType.DMA((n_expert,)),
+            pltpu.SemaphoreType.DMA((n_cuts,)),
+            pltpu.SemaphoreType.DMA((n_cuts,)),
+        ],
+        compiler_params=pltpu.CompilerParams(collective_id=0, has_side_effects=True),
+    )(values)
+    return summed[:, :width]
+
+
+def dot_nt(left, right):
+    return lax.dot_general(left, right, (((1,), (1,)), ((), ())), preferred_element_type=F32)
+
+
+def tile_of(step, size):
+    return pl.ds(pl.multiple_of(step * size, size), size)
+
+
+def lane_softmax(logits, low, high):
+    lane = lax.broadcasted_iota(jnp.int32, logits.shape, 1)
+    inside = (lane >= low) & (lane < high)
+    kept = jnp.where(inside, logits, -1e30)
+    powers = jnp.exp(kept - jnp.max(kept, axis=1, keepdims=True))
+    powers = jnp.where(inside, powers, 0.0)
+    return powers / jnp.sum(powers, axis=1, keepdims=True), lane
+
+
+def mlp_both(rows, d_rows, w_up, w_down, act, d_up, write):
+    root, cubic = math.sqrt(2.0 / math.pi), 0.044715
+
+    @pl.loop(0, act.shape[1] // 256)
+    def _(step):
+        span = tile_of(step, 256)
+        up = mm(rows[...], w_up[:, span])
+        d_act = dot_nt(d_rows[...], w_down[span, :])
+        square = up * up
+        bent = jnp.tanh(root * up * (1.0 + cubic * square))
+        half = 0.5 * (1.0 + bent)
+        act[:, span] = (up * half).astype(BF)
+        slope = half + 0.5 * up * (1.0 - bent * bent) * (root + 3.0 * root * cubic * square)
+        d_up[:, span] = (d_act * slope).astype(BF)
+
+    @pl.loop(0, w_up.shape[0] // 256)
+    def _(step):
+        span = tile_of(step, 256)
+        write(span, mm(act[...], w_down[:, span]), dot_nt(d_up[...], w_up[span, :]))
+
+
+def middle_kernel(
+    sizes, slots, second, grad_all, grad_rows, w_in, w_out, small, sort, unsort, e_in, e_out,
+    sums, returned, second_all, act_all, d_up_all, d_dense_all, rows_in, d_rows_all, act_e_all, d_first_all,
+    sec, grd, win, wout, act, d_up, d_dense, part_a, part_b, ffn_x, ffn_y, ffn_qa, ffn_qb,
+    zbuf, rows, g_rows, d_rows, act_e, d_first, wi_e, wo_e, out_a, out_b, row_x, row_y, row_qa, row_qb, sorted_back, send_back,
+    load_sem, weight_sem, store_sem, store_e_sem, z_sem, ag_sem, eag_sem, frs_sem, ers_sem, zr_sem,
+):
+    n_expert, groups, here, slab = sizes
+    me, cut = lax.axis_index("expert"), lax.axis_index("cuts")
+    at_x, at_y, at_d = (jnp.bitwise_xor(cut, k) for k in (1, 2, 3))
+    block = zbuf.shape[2]
+    per_group = here // groups
+    experts_all = n_expert * here
+
+    def load(src, dst, index):
+        copy = pltpu.make_async_copy(src, dst, load_sem.at[index])
+        copy.start()
+        return copy
+
+    def send(src, dst, sems, index, peer):
+        copy = pltpu.make_async_remote_copy(
+            src_ref=src, dst_ref=dst, send_sem=sems.at[0, index], recv_sem=sems.at[1, index],
+            device_id=peer, device_id_type=MESH,
+        )
+        copy.start()
+        return copy
+
+    loads = [
+        load(second, sec.at[cut], 0), load(w_in, win, 1), load(w_out, wout, 2), load(grad_all, grd, 3),
+    ]
+
+    def fetch_expert(i):
+        slot = i % 2
+        copies = [
+            pltpu.make_async_copy(e_in.at[i], wi_e.at[slot], weight_sem.at[0, slot]),
+            pltpu.make_async_copy(e_out.at[i], wo_e.at[slot], weight_sem.at[1, slot]),
+            pltpu.make_async_copy(grad_rows.at[i], g_rows.at[slot], weight_sem.at[2, slot]),
+        ]
+        for copy in copies:
+            copy.start()
+        return copies
+
+    fetched = [fetch_expert(0), fetch_expert(1)]
+    barrier = pltpu.get_barrier_semaphore()
+    for k in range(1, n_expert):
+        pl.semaphore_signal(barrier, inc=1, device_id=(jnp.bitwise_xor(me, k), cut), device_id_type=MESH)
+    for peer in (at_x, at_y):
+        pl.semaphore_signal(barrier, inc=1, device_id=(me, peer), device_id_type=MESH)
+    pl.semaphore_wait(barrier, n_expert + 1)
+
+    z_copies = []
+    for g in range(groups):
+        for k in range(1, n_expert):
+            peer = jnp.bitwise_xor(me, k)
+            z_copies.append(send(slots.at[g, peer], zbuf.at[g, me], z_sem, g * n_expert + k, (peer, cut)))
+    loads[0].wait()
+    ag = [
+        send(sec.at[cut], sec.at[cut], ag_sem, 0, (me, at_x)),
+        send(sec.at[cut], sec.at[cut], ag_sem, 1, (me, at_y)),
+    ]
+    for g in range(groups):
+        zbuf[g, me] = slots[g, me]
+    stores = []
+
+    def store(src, dst, index):
+        copy = pltpu.make_async_copy(src, dst, store_sem.at[index])
+        copy.start()
+        return copy
+
+    ffn_stores = {}
+
+    def ffn_block(which, owner):
+        slot = which % 2
+        if which >= 2:
+            for copy in ffn_stores[which - 2]:
+                copy.wait()
+        mixing, lane = lane_softmax(mm(sec[owner], small[...]), experts_all, experts_all + 2)
+        first_mix = jnp.sum(jnp.where(lane == experts_all, mixing, 0.0), axis=1, keepdims=True)
+        d_dense[slot] = (grd[owner].astype(F32) * first_mix).astype(BF)
+
+        def write(span, out, d_row):
+            if which == 0:
+                sums[0, :, span] = out
+                sums[1, :, span] = d_row
+            else:
+                part_a[which, :, span] = out.astype(BF)
+                part_b[which, :, span] = d_row.astype(BF)
+
+        mlp_both(sec.at[owner], d_dense.at[slot], win, wout, act.at[slot], d_up.at[slot], write)
+        ffn_stores[which] = [
+            store(act.at[slot], act_all.at[owner], 3 * which),
+            store(d_up.at[slot], d_up_all.at[owner], 3 * which + 1),
+            store(d_dense.at[slot], d_dense_all.at[owner], 3 * which + 2),
+        ]
+
+    for copy in loads[1:]:
+        copy.wait()
+    ffn_block(0, cut)
+    half = sec.shape[1] // 2
+    ag[0].wait_recv()
+    ag.append(send(sec.at[at_x, pl.ds(0, half)], sec.at[at_x, pl.ds(0, half)], ag_sem, 2, (me, at_y)))
+    ag[1].wait_recv()
+    ag.append(send(sec.at[at_y, pl.ds(half, half)], sec.at[at_y, pl.ds(half, half)], ag_sem, 3, (me, at_x)))
+    ffn_block(1, at_x)
+
+    def slab_of(owner):
+        return pl.ds(pl.multiple_of(owner * slab, slab), slab)
+
+    eag = {}
+    for g in range(groups):
+        for k in range(1, n_expert):
+            z_copies[g * (n_expert - 1) + k - 1].wait_recv()
+        flat = zbuf[g].reshape(n_expert * block, zbuf.shape[3])
+        for j in range(per_group):
+            i = g * per_group + j
+            rows[i, slab_of(cut)] = mm(sort[pl.ds(j * slab, slab), :], flat).astype(BF)
+            mine = rows.at[i, slab_of(cut)]
+            eag[i] = [
+                send(mine, mine, eag_sem, 4 * i, (me, at_x)),
+                send(mine, mine, eag_sem, 4 * i + 1, (me, at_y)),
+            ]
+    ffn_block(2, at_y)
+    ag[2].wait_recv()
+    ag[3].wait_recv()
+
+    def relay(i):
+        cut_half = slab // 2
+        eag[i][0].wait_recv()
+        piece = rows.at[i, pl.ds(pl.multiple_of(at_x * slab, slab), cut_half)]
+        eag[i].append(send(piece, piece, eag_sem, 4 * i + 2, (me, at_y)))
+        eag[i][1].wait_recv()
+        piece = rows.at[i, pl.ds(pl.multiple_of(at_y * slab + cut_half, cut_half), cut_half)]
+        eag[i].append(send(piece, piece, eag_sem, 4 * i + 3, (me, at_x)))
+
+    relay(0)
+    ffn_block(3, at_d)
+    frs = [
+        send(part_a.at[1], ffn_x.at[0], frs_sem, 0, (me, at_x)),
+        send(part_a.at[3], ffn_x.at[1], frs_sem, 1, (me, at_x)),
+        send(part_b.at[2], ffn_y.at[0], frs_sem, 2, (me, at_y)),
+        send(part_b.at[3], ffn_y.at[1], frs_sem, 3, (me, at_y)),
+    ]
+    second_store = store(sec, second_all, 12)
+    expert_stores = {}
+    ers = {}
+
+    def expert(i):
+        slot = i % 2
+        if i >= 2:
+            for copy in expert_stores[i - 2]:
+                copy.wait()
+        for copy in fetched[i]:
+            copy.wait()
+        logits = mm(rows[i], small[...])
+        router, lane = lane_softmax(logits, 0, experts_all)
+        gate = jnp.sum(jnp.where(lane == me * here + i, router, 0.0), axis=1, keepdims=True)
+        mixing, lane = lane_softmax(logits, experts_all, experts_all + 2)
+        mixing = jnp.sum(jnp.where(lane == experts_all + 1, mixing, 0.0), axis=1, keepdims=True)
+        d_rows[slot] = (g_rows[slot].astype(F32) * mixing * gate).astype(BF)
+
+        def write(span, out, d_row):
+            out_a[i, :, span] = out.astype(BF)
+            out_b[i, :, span] = d_row.astype(BF)
+
+        mlp_both(rows.at[i], d_rows.at[slot], wi_e.at[slot], wo_e.at[slot], act_e.at[slot], d_first.at[slot], write)
+        expert_stores[i] = []
+        for n, (src, dst) in enumerate(((d_rows, d_rows_all), (act_e, act_e_all), (d_first, d_first_all))):
+            copy = pltpu.make_async_copy(src.at[slot], dst.at[i], store_e_sem.at[n, slot])
+            copy.start()
+            expert_stores[i].append(copy)
+        ers[i] = [
+            send(out_a.at[i, slab_of(at_x)], row_x.at[i, 0], ers_sem, 6 * i, (me, at_x)),
+            send(out_a.at[i, slab_of(at_d)], row_x.at[i, 1], ers_sem, 6 * i + 1, (me, at_x)),
+            send(out_b.at[i, slab_of(at_y)], row_y.at[i, 0], ers_sem, 6 * i + 2, (me, at_y)),
+            send(out_b.at[i, slab_of(at_d)], row_y.at[i, 1], ers_sem, 6 * i + 3, (me, at_y)),
+        ]
+
+    def add_into(ref, *others):
+        total = ref[...].astype(F32)
+        for other in others:
+            total = total + other[...].astype(F32)
+        ref[...] = total.astype(BF)
+
+    def pass_on(i):
+        for copy in ers[i][:4]:
+            copy.wait_recv()
+        add_into(out_a.at[i, slab_of(at_y)], row_x.at[i, 1])
+        add_into(out_b.at[i, slab_of(at_x)], row_y.at[i, 1])
+        ers[i] += [
+            send(out_a.at[i, slab_of(at_y)], row_qa.at[i], ers_sem, 6 * i + 4, (me, at_y)),
+            send(out_b.at[i, slab_of(at_x)], row_qb.at[i], ers_sem, 6 * i + 5, (me, at_x)),
+        ]
+
+    back_copies = []
+
+    def finish(i):
+        ers[i][4].wait_recv()
+        ers[i][5].wait_recv()
+        for n, (out, near, far) in enumerate(((out_a, row_x, row_qa), (out_b, row_y, row_qb))):
+            total = out[i, slab_of(cut)].astype(F32) + near[i, 0].astype(F32) + far[i].astype(F32)
+            sorted_back[n, i] = total.astype(BF)
+        if (i + 1) % per_group == 0:
+            g = i // per_group
+            for n in range(2):
+                flat = sorted_back[n, pl.ds(g * per_group, per_group)].reshape(per_group * slab, -1)
+                placed = mm(unsort[...], flat).astype(BF)
+                send_back[n, g] = placed.reshape(n_expert, block, -1)
+                returned[n, g, me] = send_back[n, g, me]
+                for k in range(1, n_expert):
+                    peer = jnp.bitwise_xor(me, k)
+                    back_copies.append(
+                        send(
+                            send_back.at[n, g, peer], returned.at[n, g, me], zr_sem,
+                            (n * groups + g) * n_expert + k, (peer, cut),
+                        )
+                    )
+
+    for i in range(here):
+        if i + 1 < here:
+            relay(i + 1)
+        eag[i][2].wait_recv()
+        eag[i][3].wait_recv()
+        expert(i)
+        if i + 2 < here:
+            fetched.append(fetch_expert(i + 2))
+        if i == 0:
+            for copy in frs[:4]:
+                copy.wait_recv()
+            add_into(part_a.at[2], ffn_x.at[1])
+            add_into(part_b.at[1], ffn_y.at[1])
+            frs += [
+                send(part_a.at[2], ffn_qa, frs_sem, 4, (me, at_y)),
+                send(part_b.at[1], ffn_qb, frs_sem, 5, (me, at_x)),
+            ]
+        if i >= 1:
+            pass_on(i - 1)
+        if i >= 2:
+            finish(i - 2)
+    rows_store = store(rows, rows_in, 13)
+    pass_on(here - 1)
+    finish(here - 2)
+    frs[4].wait_recv()
+    frs[5].wait_recv()
+    sums[0] = sums[0] + ffn_x[0].astype(F32) + ffn_qa[...].astype(F32)
+    sums[1] = sums[1] + ffn_y[0].astype(F32) + ffn_qb[...].astype(F32)
+    finish(here - 1)
+    for copy in back_copies:
+        copy.wait_recv()
+    for copy in z_copies + ag + frs + back_copies:
+        copy.wait_send()
+    for i in range(here):
+        for copy in eag[i] + ers[i]:
+            copy.wait_send()
+    for which in (2, 3):
+        for copy in ffn_stores[which]:
+            copy.wait()
+    for i in (here - 2, here - 1):
+        for copy in expert_stores[i]:
+            copy.wait()
+    second_store.wait()
+    rows_store.wait()
+
+
+def middle(slots, second, grad_all, grad_rows, w_in, w_out, small, sort, unsort, e_in, e_out, n_expert, n_cuts):
+    groups, _, block, width = slots.shape
+    tokens = second.shape[0]
+    here, _, hidden = e_in.shape
+    ffn = w_in.shape[1]
+    slab = n_expert * block * groups // here
+    rows = n_cuts * slab
+    any_spec, vmem_spec = pl.BlockSpec(memory_space=pl.ANY), pl.BlockSpec(memory_space=pltpu.VMEM)
+    shape = jax.ShapeDtypeStruct
+    dma = pltpu.SemaphoreType.DMA
+    flops = 8 * (n_cuts * tokens * ffn + here * rows * hidden) * width
+    return pl.pallas_call(
+        functools.partial(middle_kernel, (n_expert, groups, here, slab)),
+        name="middle",
+        out_shape=(
+            shape((2, tokens, width), F32), shape((2, groups, n_expert, block, width), BF),
+            shape((n_cuts, tokens, width), BF), shape((n_cuts, tokens, ffn), BF),
+            shape((n_cuts, tokens, ffn), BF), shape((n_cuts, tokens, width), BF),
+            shape((here, rows, width), BF), shape((here, rows, width), BF),
+            shape((here, rows, hidden), BF), shape((here, rows, hidden), BF),
+        ),
+        in_specs=[vmem_spec] + [any_spec] * 5 + [vmem_spec] * 3 + [any_spec] * 2,
+        out_specs=(vmem_spec,) * 2 + (any_spec,) * 8,
+        scratch_shapes=[
+            pltpu.VMEM((n_cuts, tokens, width), BF), pltpu.VMEM((n_cuts, tokens, width), BF),
+            pltpu.VMEM((width, ffn), BF), pltpu.VMEM((ffn, width), BF),
+            pltpu.VMEM((2, tokens, ffn), BF), pltpu.VMEM((2, tokens, ffn), BF), pltpu.VMEM((2, tokens, width), BF),
+            pltpu.VMEM((n_cuts, tokens, width), BF), pltpu.VMEM((n_cuts, tokens, width), BF),
+            pltpu.VMEM((2, tokens, width), BF), pltpu.VMEM((2, tokens, width), BF),
+            pltpu.VMEM((tokens, width), BF), pltpu.VMEM((tokens, width), BF),
+            pltpu.VMEM((groups, n_expert, block, width), BF), pltpu.VMEM((here, rows, width), BF),
+            pltpu.VMEM((2, rows, width), BF), pltpu.VMEM((2, rows, width), BF),
+            pltpu.VMEM((2, rows, hidden), BF), pltpu.VMEM((2, rows, hidden), BF),
+            pltpu.VMEM((2, width, hidden), BF), pltpu.VMEM((2, hidden, width), BF),
+            pltpu.VMEM((here, rows, width), BF), pltpu.VMEM((here, rows, width), BF),
+            pltpu.VMEM((here, 2, slab, width), BF), pltpu.VMEM((here, 2, slab, width), BF),
+            pltpu.VMEM((here, slab, width), BF), pltpu.VMEM((here, slab, width), BF),
+            pltpu.VMEM((2, here, slab, width), BF), pltpu.VMEM((2, groups, n_expert, block, width), BF),
+            dma((4,)), dma((3, 2)), dma((14,)), dma((3, 2)),
+            dma((2, groups * n_expert)), dma((2, 4)), dma((2, 4 * here)), dma((2, 6)), dma((2, 6 * here)),
+            dma((2, 2 * groups * n_expert)),
+        ],
+        compiler_params=pltpu.CompilerParams(
+            collective_id=1, has_side_effects=True, vmem_limit_bytes=67_000_000
+        ),
+        cost_estimate=pl.CostEstimate(flops=flops, bytes_accessed=48 << 20, transcendentals=0),
+    )(slots, second, grad_all, grad_rows, w_in, w_out, small, sort, unsort, e_in, e_out)
 
 
 def shards(
@@ -83,6 +525,32 @@
     experts_here = expert_in.shape[0]
     capacity = 3 * tokens // (2 * experts_all)
 
+    onehot = (routes[:, None] == jnp.arange(experts_all, dtype=jnp.int32)[None, :]).astype(F32)
+    onehot_kept = onehot * kept_mask.astype(F32)[:, None]
+    lower_tri = (jnp.arange(tokens)[:, None] >= jnp.arange(tokens)[None, :]).astype(BF)
+    running = mm(lower_tri, onehot_kept.astype(BF))
+    slot_num = jnp.sum(onehot_kept * running, axis=1) - 1.0
+    fused = n_cuts == 4
+    groups = 2 if fused else 1
+    per_group = experts_here // groups
+    block = per_group * capacity
+    owner, local = routes // experts_here, routes % experts_here
+    start = (local // per_group) * (n_expert * block) + owner * block + local % per_group * capacity
+    target = start.astype(F32) + slot_num
+    columns = jnp.arange(experts_all * capacity, dtype=jnp.int32).astype(F32)
+    placer = ((columns[None, :] == target[:, None]) & (kept_mask[:, None] > 0)).astype(BF)
+
+    def to_owners(rows):
+        grid = mm_tn(placer, rows).astype(BF).reshape(groups, n_expert, block, features)
+        grid = grid.swapaxes(0, 1).reshape(n_expert, experts_here, capacity, features)
+        moved = lax.all_to_all(grid, "expert", split_axis=0, concat_axis=2, tiled=True)
+        return lax.all_gather(moved, "cuts", axis=2, tiled=True)[0]
+
+    def to_sources(rows):
+        summed = lax.psum_scatter(rows[None].astype(BF), "cuts", scatter_dimension=2, tiled=True)
+        moved = lax.all_to_all(summed, "expert", split_axis=2, concat_axis=0, tiled=True)
+        return mm(placer, moved.reshape(-1, features))
+
     gains = gather_cuts(jnp.stack([gain_attn, gain_ffn], axis=1)).astype(F32)
     gain_one, gain_two = gains[:, 0], gains[:, 1]
     inputs = block_input.astype(F32)
@@ -111,63 +579,78 @@
     head_out = rows_to_cuts(heads_here.reshape(seq_len, own).astype(BF))
     attn_full = gather_cuts(w_attn_out)
     small_full = gather_cuts(jnp.concatenate([w_router, w_mix], axis=1))
+    grad_all = gather_cuts(cotangent)
+    grad_rows = to_owners(cotangent)
+    in_here = columns_to_cuts(w_in)
     hidden = inputs + mm(head_out, attn_full)
     xhat_two, inv_two = norm_parts(hidden)
     second = (xhat_two * gain_two).astype(BF)
 
     logits = mm(second, small_full)
-    onehot = (routes[:, None] == jnp.arange(experts_all, dtype=jnp.int32)[None, :]).astype(F32)
     router_p = softmax_rows(logits[:, :experts_all])
     mixing = softmax_rows(logits[:, experts_all:])
     gate = jnp.sum(router_p * onehot, axis=1)
     grad = cotangent.astype(F32)
-    d_dense = (grad * mixing[:, 0:1]).astype(BF)
     d_moe = grad * mixing[:, 1:2]
-    d_picked = (d_moe * gate[:, None]).astype(BF)
-
-    onehot_kept = onehot * kept_mask.astype(F32)[:, None]
-    lower_tri = (jnp.arange(tokens)[:, None] >= jnp.arange(tokens)[None, :]).astype(BF)
-    running = mm(lower_tri, onehot_kept.astype(BF))
-    slot_num = jnp.sum(onehot_kept * running, axis=1) - 1.0
-    target = routes.astype(F32) * capacity + slot_num
-    columns = jnp.arange(experts_all * capacity, dtype=jnp.int32).astype(F32)
-    placer = ((columns[None, :] == target[:, None]) & (kept_mask[:, None] > 0)).astype(BF)
-    both = jnp.concatenate([second, d_picked], axis=1)
-    slots = mm_tn(placer, both).astype(BF)
-    grid = slots.reshape(n_expert, experts_here, capacity, 2 * features)
-    moved = lax.all_to_all(grid, "expert", split_axis=0, concat_axis=2, tiled=True)
-    rows_both = lax.all_gather(moved, "cuts", axis=2, tiled=True)[0]
-    rows_in, d_rows = rows_both[:, :, :features], rows_both[:, :, features:]
-
-    ffn_both = gather_cuts(jnp.concatenate([second, d_dense], axis=1))
-    second_all, d_dense_all = ffn_both[:, :features], ffn_both[:, features:]
-    in_here = columns_to_cuts(w_in)
-    up_proj = mm(second_all, in_here)
-    activ, gelu_pull = jax.vjp(jax.nn.gelu, up_proj)
-    activ_low = activ.astype(BF)
-    dense_part = mm(activ_low, w_out)
-    d_activ = mm_nt(d_dense_all, w_out)
-    g_out = mm_tn(activ_low, d_dense_all)
-    d_up = gelu_pull(d_activ)[0].astype(BF)
-    g_in = mm_tn(second_all, d_up)
-    d_second_part = mm_nt(d_up, in_here)
-    ffn_sums = scatter_cuts(jnp.concatenate([dense_part, d_second_part], axis=1))
-    dense, d_second_ffn = ffn_sums[:, :features].astype(F32), ffn_sums[:, features:].astype(F32)
-
-    first = jnp.einsum("erd,edh->erh", rows_in, expert_in, preferred_element_type=F32)
-    expert_act, expert_pull = jax.vjp(jax.nn.gelu, first)
-    expert_low = expert_act.astype(BF)
-    partial_out = jnp.einsum("erh,ehd->erd", expert_low, expert_out, preferred_element_type=F32)
-    d_expert_act = jnp.einsum("erd,ehd->erh", d_rows, expert_out, preferred_element_type=F32)
-    d_first = expert_pull(d_expert_act)[0].astype(BF)
-    d_rows_in = jnp.einsum("erh,edh->erd", d_first, expert_in, preferred_element_type=F32)
-    g_expert_out = jnp.einsum("erh,erd->ehd", expert_low, d_rows, preferred_element_type=F32)
-    g_expert_in = jnp.einsum("erd,erh->edh", rows_in, d_first, preferred_element_type=F32)
-    back = jnp.concatenate([partial_out, d_rows_in], axis=2).astype(BF)
-    summed = lax.psum_scatter(back[None], "cuts", scatter_dimension=2, tiled=True)
-    returned = lax.all_to_all(summed, "expert", split_axis=2, concat_axis=0, tiled=True)
-    picked_both = mm(placer, returned.reshape(-1, 2 * features))
-    picked, d_picked_in = picked_both[:, :features], picked_both[:, features:]
+
+    if fused:
+        slots = mm_tn(placer, second).astype(BF).reshape(groups, n_expert, block, features)
+        width = n_expert * block
+        at = jnp.arange(width, dtype=jnp.int32)
+        slab = n_expert * capacity
+        goal = at % slab // capacity * block + at // slab * capacity + at % capacity
+        sort = (goal[:, None] == at[None, :]).astype(BF)
+        small_wide = jnp.pad(small_full, ((0, 0), (0, -small_full.shape[1] % 128)))
+        sums, returned, second_all, activ_low, d_up, d_dense_all, rows_in, d_rows, expert_low, d_first = middle(
+            slots, second, grad_all.reshape(n_cuts, tokens, features), grad_rows, in_here, w_out, small_wide,
+            sort, sort.T, expert_in, expert_out, n_expert, n_cuts,
+        )
+        dense, d_second_ffn = sums[0], sums[1]
+        second_all, activ_low, d_up, d_dense_all = (
+            v.reshape(seq_len, -1) for v in (second_all, activ_low, d_up, d_dense_all)
+        )
+        g_out = mm_tn(activ_low, d_dense_all)
+        g_in = mm_tn(second_all, d_up)
+        g_expert_out = jnp.einsum("erh,erd->ehd", expert_low, d_rows, preferred_element_type=F32)
+        g_expert_in = jnp.einsum("erd,erh->edh", rows_in, d_first, preferred_element_type=F32)
+        picked = mm(placer, returned[0].reshape(-1, features))
+        d_picked_in = mm(placer, returned[1].reshape(-1, features))
+    else:
+        rows_in = to_owners(second)
+        row_logits = jnp.einsum("erd,dk->erk", rows_in, small_full, preferred_element_type=F32)
+        ids = lax.axis_index("expert") * experts_here + jnp.arange(experts_here, dtype=jnp.int32)
+        is_here = (jnp.arange(experts_all, dtype=jnp.int32)[None, :] == ids[:, None]).astype(F32)
+        row_gate = jnp.sum(
+            softmax_rows(row_logits[:, :, :experts_all]) * is_here[:, None, :], axis=2, keepdims=True
+        )
+        row_mixing = softmax_rows(row_logits[:, :, experts_all:])[:, :, 1:2]
+        d_rows = (grad_rows.astype(F32) * row_mixing * row_gate).astype(BF)
+
+        first = jnp.einsum("erd,edh->erh", rows_in, expert_in, preferred_element_type=F32)
+        expert_act, expert_pull = jax.vjp(jax.nn.gelu, first)
+        expert_low = expert_act.astype(BF)
+        partial_out = jnp.einsum("erh,ehd->erd", expert_low, expert_out, preferred_element_type=F32)
+        picked = to_sources(partial_out)
+
+        second_all = gather_cuts(second)
+        mixing_all = softmax_rows(mm(second_all, small_full[:, experts_all:]))
+        d_dense_all = (grad_all.astype(F32) * mixing_all[:, 0:1]).astype(BF)
+        up_proj = mm(second_all, in_here)
+        activ, gelu_pull = jax.vjp(jax.nn.gelu, up_proj)
+        activ_low = activ.astype(BF)
+        dense = scatter_cuts(mm(activ_low, w_out)).astype(F32)
+        d_activ = mm_nt(d_dense_all, w_out)
+        g_out = mm_tn(activ_low, d_dense_all)
+        d_up = gelu_pull(d_activ)[0].astype(BF)
+        g_in = mm_tn(second_all, d_up)
+        d_second_ffn = scatter_cuts(mm_nt(d_up, in_here)).astype(F32)
+
+        d_expert_act = jnp.einsum("erd,ehd->erh", d_rows, expert_out, preferred_element_type=F32)
+        d_first = expert_pull(d_expert_act)[0].astype(BF)
+        d_rows_in = jnp.einsum("erh,edh->erd", d_first, expert_in, preferred_element_type=F32)
+        g_expert_out = jnp.einsum("erh,erd->ehd", expert_low, d_rows, preferred_element_type=F32)
+        g_expert_in = jnp.einsum("erd,erh->edh", rows_in, d_first, preferred_element_type=F32)
+        d_picked_in = to_sources(d_rows_in)
 
     moe_val = gate[:, None] * picked
     block_out = (hidden + mixing[:, 0:1] * dense + mixing[:, 1:2] * moe_val).astype(BF)
@@ -176,7 +659,7 @@
     d_router = router_p * (onehot - gate[:, None]) * d_gate[:, None]
     d_mix = mixing * (d_mixing - jnp.sum(mixing * d_mixing, axis=1, keepdims=True))
     d_small = jnp.concatenate([d_router, d_mix], axis=1).astype(BF)
-    g_small = mm_tn(second, d_small)
+    g_small = mm_tn(d_small, second)
     d_second = d_second_ffn + mm_nt(d_small, small_full) + d_picked_in
     d_hidden_norm, g_gain_two = norm_back(d_second, xhat_two, inv_two, gain_two)
     d_hidden = grad + d_hidden_norm
@@ -212,11 +695,12 @@
         s_qkv.reshape(deep, 3, 1, own), "cuts", split_axis=0, concat_axis=2, tiled=True
     )
     s_qkv = s_qkv.reshape(-1, 3 * features).astype(F32)
-    s_attn_out = lax.psum_scatter(
-        g_attn_out.astype(BF), ("expert", "cuts"), scatter_dimension=0, tiled=True
-    ).astype(F32)
-    tiny = jnp.concatenate([g_small, g_gain_one[:, None], g_gain_two[:, None]], axis=1)
-    s_tiny = lax.psum_scatter(tiny, ("expert", "cuts"), scatter_dimension=0, tiled=True)
+    s_attn_out = scatter_cuts(over_experts(g_attn_out)).astype(F32)
+    tiny = jnp.concatenate([g_small, g_gain_one[None, :], g_gain_two[None, :]], axis=0)
+    tiny = jnp.pad(tiny, ((0, -tiny.shape[0] % 8), (0, 0)))
+    tiny = sum_small(tiny, n_expert, n_cuts)
+    width = features // (n_expert * n_cuts)
+    s_tiny = lax.dynamic_slice_in_dim(tiny, lax.axis_index("cuts") * width, width, axis=1)
     return (
         block_out,
         d_block_input,
@@ -224,10 +708,10 @@
         s_attn_out,
         s_in,
         s_out,
-        s_tiny[:, :experts_all],
-        s_tiny[:, experts_all : experts_all + 2],
-        s_tiny[:, experts_all + 2],
-        s_tiny[:, experts_all + 3],
+        s_tiny[:experts_all].T,
+        s_tiny[experts_all : experts_all + 2].T,
+        s_tiny[experts_all + 2],
+        s_tiny[experts_all + 3],
         g_expert_in,
         g_expert_out,
     )

time: 897 us -> 661 us (0.74)
  waiting for transfers between devices: 455 us -> 256 us
  Pallas kernels: 0 us -> 168 us
  blocking collectives: 109 us -> 24.8 us
  matrix products: 159 us -> 100 us
  local copies, waits for them, and re-layouts: 55.3 us -> 30.1 us
  other arithmetic: 49.7 us -> 31 us
  starting transfers between devices: 41.2 us -> 30 us
    pallas_call x0 -> x2, Pallas kernels: none -> 168 us  [the longest x1 155 us: middle(): pl.pallas_call(functools.partial(middle_kernel, (n_expert, groups, here,...]
    reduce_scatter x2 -> x0, waiting for transfers between devices: 139 us -> none  [the longest x1 114 us: shards(): lax.psum_scatter(g_attn_out.astype(BF), ('expert', 'cuts'), scatter_dimen...]
    unnamed x13 -> x10, waiting for transfers between devices: 134 us -> 1.51 us
    all_to_all x2 -> x0, blocking collectives: 85.9 us -> none  [the longest x1 43.7 us: columns_to_cuts(): return lax.all_to_all(rows, 'cuts', split_axis=1, concat_axis=0, tiled=True)]
    reduce_scatter x3 -> x4, waiting for transfers between devices: 8.18 us -> 90.3 us  [over_experts(): lax.psum_scatter(part.astype(BF), 'expert', scatter_dimension=0, tiled=True)]
    dot_general x4 -> x0, matrix products: 39.3 us -> none  [the longest x1 13 us: shards(): jnp.einsum('erd,ehd->erh', d_rows, expert_out, preferred_element_type=F32)]
    all_to_all x1 -> x2, waiting for transfers between devices: 0.87 us -> 34.3 us  [columns_to_cuts(): return lax.all_to_all(rows, 'cuts', split_axis=1, concat_axis=0, tiled=True)]
    all_gather x1, waiting for transfers between devices: 65.3 us -> 43.4 us  [to_owners(): return lax.all_gather(moved, 'cuts', axis=2, tiled=True)[0]]
  transfers between devices with their start and end apart: 19 -> 18, of which waited for: 14 -> 11; matrix products, arithmetic and copies ran while one was open for 26% -> 15% of each run, Pallas kernels for 0% -> 2%
where the time goes in v2:
time: 661 us; the launch traced here: 656 us
  waiting for transfers between devices  256 us (39%)
  Pallas kernels  168 us (25%)
  matrix products  100 us (15%)
  other arithmetic  31 us (5%)
  local copies, waits for them, and re-layouts  30.1 us (5%)
  starting transfers between devices  30 us (5%)
  blocking collectives  24.8 us (4%)
  between operations  15.8 us (2%)
    pallas_call x1, Pallas kernels, middle(): pl.pallas_call(functools.partial(middle_kernel, (n_expert, groups, here,...  155 us
    reduce_scatter x4, waiting for transfers between devices, over_experts(): lax.psum_scatter(part.astype(BF), 'expert', scatter_dimension=0, tiled=True)  90.3 us
    all_gather x1, waiting for transfers between devices, to_owners(): return lax.all_gather(moved, 'cuts', axis=2, tiled=True)[0]  43.4 us
    reduce_scatter x2, waiting for transfers between devices, scatter_cuts(): lax.psum_scatter(rows.astype(BF), 'cuts', scatter_dimension=0, tiled=True)  42.3 us
    all_to_all x2, waiting for transfers between devices, columns_to_cuts(): return lax.all_to_all(rows, 'cuts', split_axis=1, concat_axis=0, tiled=True)  34.3 us
    all_gather x2, blocking collectives, gather_cuts(): return lax.all_gather(rows, 'cuts', axis=0, tiled=True)  24.8 us
    all_to_all x1, waiting for transfers between devices, shards(): lax.all_to_all(w_qkv.reshape(own, 3, n_cuts, own), 'cuts', split_axis=2,...  20.3 us
    dot_general x7, matrix products, mm_tn(): lax.dot_general(left, right, (((0,), (0,)), ((), ())), preferred_element_...  19.2 us
  transfers between devices with their start and end apart: 18, of which 11 were waited for; matrix products, arithmetic and copies ran while one was open for 15% of the time, Pallas kernels for 2%

profile of v2, /device:TPU:0, one launch (start us, length us, event | category | flops | bytes accessed | tf_op | source)
XLA Modules:
  0.0 656.3 jit_solution(7212669265190710701)
XLA Ops:
  11.2 9.6 %all_gather.18 = bf16[1024,2]{0,1:T(2,128)(2,1)S(1)} all-gather(bf16[256,2]{0,1:T(2,128)(2,1)S(1)} %pad_maximum_fusion.5), channel_id=1, replica_groups=mesh['expert'=8,'cuts'=4] {'cuts'}, dimensions={0}, use_global_device_ids=true | all-gather | bytes 5120 | tf_op jit(solution)/shard_map/all_gather | solution.py:50
  33.5 20.3 %all-to-all-done = bf16[256,3,4,256]{0,3,1,2:T(8,128)(2,1)S(1)} async-done(((bf16[256,3,4,256]{0,3,1,2:T(8,128)(2,1)}), bf16[256,3,4,256]{0,3,1,2:T(8,128)(2,1)S(1)}, u32[]{:S(2)}, u32[]{:S(2)}) %all-to-all-start) | async-done | bytes 1572896 | tf_op jit(solution)/shard_map/all_to_all | solution.py:559
  60.9 18.8 %all-to-all-done.2 = bf16[8,4,12,1024]{3,1,2,0:T(4,128)(2,1)S(1)} async-done(((bf16[8,4,12,1024]{3,1,2,0:T(4,128)(2,1)}), bf16[8,4,12,1024]{3,1,2,0:T(4,128)(2,1)S(1)}, u32[]{:S(2)}, u32[]{:S(2)}) %all-to-all-start.2) | async-done | bytes 786464 | tf_op jit(solution)/shard_map/all_to_all | solution.py:546
  84.3 7.8 %fusion.73 = (f32[4,1024]{1,0:T(4,128)S(1)}, f32[4,1024,1024]{1,2,0:T(8,128)}) fusion(bf16[1024,3,4,64]{0,3,2,1:T(8,128)(2,1)S(1)} %bitcast.163, pred[1024,1024]{0,1:T(8,128)(4,1)S(1)} %iota_compare_fusion), kind=kOutput, calls=%fused_computation.171 | convolution fusion | flops 549449728 | bytes 18890752 | tf_op jit(solution)/shard_map/qhd,khd->hqk/dot_general | solution.py:569
  92.1 8.3 %fusion = f32[4,1024]{1,0:T(4,128)S(1)} fusion(f32[4,1024,1024]{1,2,0:T(8,128)} %get-tuple-element.137, f32[4,1024]{1,0:T(4,128)S(1)} %get-tuple-element.136), kind=kLoop, calls=%fused_computation.6 | loop fusion | flops 8384512 | bytes 16809984 | tf_op jit(solution)/shard_map/reduce_sum | solution.py:575
  101.1 7.4 %fusion.19 = bf16[1024,4,64]{0,2,1:T(8,128)(2,1)S(1)} fusion(f32[4,1024,1024]{1,2,0:T(8,128)} %get-tuple-element.137, f32[4,1024]{1,0:T(4,128)S(1)} %fusion, f32[4,1024]{1,0:T(4,128)S(1)} %get-tuple-element.136, bf16[1024,3,4,64]{0,3,2,1:T(8,128)(2,1)S(1)} %bitcast.164), kind=kOutput, calls=%fused_computation.47 | convolution fusion | flops 549715968 | bytes 17858560 | tf_op jit(solution)/shard_map/hqk,khd->qhd/dot_general | solution.py:577
  114.9 15.2 %all_gather.21 = bf16[1024,34]{1,0:T(8,128)(2,1)S(1)} all-gather(bf16[256,34]{1,0:T(8,128)(2,1)S(1)} %copy.160), channel_id=1, replica_groups=mesh['expert'=8,'cuts'=4] {'cuts'}, dimensions={0}, use_global_device_ids=true | all-gather | bytes 87040 | tf_op jit(solution)/shard_map/all_gather | solution.py:50
  143.5 25.5 %all-to-all-done.3 = bf16[256,4,1024]{2,0,1:T(8,128)(2,1)} async-done(((bf16[256,4,1024]{2,0,1:T(8,128)(2,1)}), bf16[256,4,1024]{2,0,1:T(8,128)(2,1)}, u32[]{:S(2)}, u32[]{:S(2)}) %all-to-all-start.3) | async-done | bytes 2097184 | tf_op jit(solution)/shard_map/all_to_all | solution.py:58
  169.0 43.4 %all-gather.11.cloned.1.call-done = bf16[1,4,384,1024]{3,2,1,0:T(8,128)(2,1)} async-done(((bf16[1,4,96,1024]{3,2,1,0:T(8,128)(2,1)}), bf16[1,4,384,1024]{3,2,1,0:T(8,128)(2,1)}) %all-gather.11.cloned.1.call-update) | async-done | bytes 3145744 | tf_op jit(solution)/shard_map/all_gather | solution.py:547
  212.3 155.4 %middle.1 = (f32[2,256,1024]{2,1,0:T(8,128)}, bf16[2,2,8,24,1024]{4,3,2,1,0:T(8,128)(2,1)}, bf16[4,256,1024]{2,1,0:T(8,128)(2,1)}, bf16[4,256,1024]{2,1,0:T(8,12...) custom-call(bf16[2,8,24,1024]{3,2,1,0:T(8,128)(2,1)} %bitcast.174, ...), custom_call_target="tpu_custom_call" | custom-call | flops 21474836480 | bytes 50331648 | tf_op jit(solution)/shard_map/middle/pallas_call | solution.py:463
  380.8 8.9 %all-to-all-done.4 = bf16[256,4,256]{2,0,1:T(8,128)(2,1)S(1)} async-done(((bf16[256,4,256]{2,0,1:T(8,128)(2,1)}), bf16[256,4,256]{2,0,1:T(8,128)(2,1)S(1)}, u32[]{:S(2)}, u32[]{:S(2)}) %all-to-all-start.4) | async-done | bytes 524320 | tf_op jit(solution)/shard_map/all_to_all | solution.py:58
  390.4 8.6 %fusion.6 = bf16[1024,1,4,64]{0,3,2,1:T(8,128)(2,1)S(1)} fusion(bf16[1024,4,64]{0,2,1:T(8,128)(2,1)S(1)} %reshape.213, f32[4,1024,1024]{1,2,0:T(8,128)} %get-tuple-element.137, f32[4,1024]{1,0:T(4,128)S(1)} %log_add_fusion), kind=kOutput, calls=%fused_computation.29 | convolution fusion | flops 545259520 | bytes 17842176 | tf_op jit(solution)/shard_map/hqk,qhd->khd/dot_general | solution.py:676
  399.0 13.1 %multiply_reduce_fusion = (f32[4,1024]{1,0:T(4,128)S(1)}, f32[4,1024,1024]{1,2,0:T(8,128)}) fusion(f32[4,1024,1024]{1,2,0:T(8,128)} %get-tuple-element.137, f32[4,1024]{1,0:T(4,128)S(1)} %log_add_fusion, bf16[1024,4,64]{0,2,1:T(8,128)(2,1)S(1)} %reshape.213, bf16[1024,3,4,64]{0,3,2,1:T(8,128)(2,1)} %bitcast.165), kind=kOutput, calls=%fused_computation.1 | convolution fusion | flops 549449728 | bytes 34635776 | tf_op jit(solution)/shard_map/qhd,khd->hqk/dot_general | solution.py:671
  412.1 7.8 %multiply_convert_fusion = bf16[4,1024,1024]{1,2,0:T(8,128)(2,1)S(1)} fusion(f32[4,1024,1024]{1,2,0:T(8,128)} %get-tuple-element.142, f32[4,1024,1024]{1,2,0:T(8,128)S(1)} %bitcast.150, f32[4,1024]{1,0:T(4,128)S(1)} %get-tuple-element.141, f32[4,1024]{1,0:T(4,128)S(1)} %log_add_fusion), kind=kLoop, calls=%fused_computation | loop fusion | flops 16777216 | bytes 41975808 | tf_op jit(solution)/shard_map/convert_element_type | solution.py:673
  431.7 5.9 bitcast_convert_fusion.1
  437.9 5.9 bitcast_convert_fusion
  451.7 13.7 %fusion.76 = f32[4,1024,1024]{2,1,0:T(8,128)} fusion(bf16[4,384,1024]{2,1,0:T(8,128)(2,1)} %get-tuple-element.28, bf16[4,384,1024]{2,1,0:T(8,128)(2,1)} %get-tuple-element.29), kind=kOutput, calls=%fused_computation.174 | convolution fusion | flops 3221225472 | bytes 23068672 | tf_op jit(solution)/shard_map/erd,erh->edh/dot_general | solution.py:615
  465.4 8.6 %fusion.77 = f32[4,1024,1024]{2,1,0:T(8,128)} fusion(bf16[4,384,1024]{2,1,0:T(8,128)(2,1)S(1)} %copy-done.14, bf16[4,384,1024]{2,1,0:T(8,128)(2,1)S(1)} %copy-done.13), kind=kOutput, calls=%fused_computation.175 | convolution fusion | flops 3221225472 | bytes 23068672 | tf_op jit(solution)/shard_map/erh,erd->ehd/dot_general | solution.py:614
  484.9 15.9 %reduce-scatter.15.cloned.1.call-done = bf16[128,1024]{1,0:T(8,128)(2,1)} async-done(((bf16[1024,1024]{1,0:T(8,128)(2,1)}), bf16[128,1024]{1,0:T(8,128)(2,1)}) %reduce-scatter.15.cloned.1.call-update) | async-done | bytes 262160 | tf_op jit(solution)/shard_map/reduce_scatter | solution.py:684
  504.5 33.2 %reduce-scatter.17.cloned.1.call-done = bf16[128,1024]{1,0:T(8,128)(2,1)} async-done(((bf16[1024,1024]{1,0:T(8,128)(2,1)}), bf16[128,1024]{1,0:T(8,128)(2,1)}) %reduce-scatter.17.cloned.1.call-update) | async-done | bytes 262160 | tf_op jit(solution)/shard_map/reduce_scatter | solution.py:684
  540.6 41.3 %reduce-scatter.11.cloned.1.call-done = bf16[128,1024]{1,0:T(8,128)(2,1)} async-done(((bf16[1024,1024]{1,0:T(8,128)(2,1)}), bf16[128,1024]{1,0:T(8,128)(2,1)}) %reduce-scatter.11.cloned.1.call-update) | async-done | bytes 262160 | tf_op jit(solution)/shard_map/reduce_scatter | solution.py:684
  583.6 36.9 %reduce-scatter.7.cloned.1.call-done = bf16[256,1024]{1,0:T(8,128)(2,1)} async-done(((bf16[1024,1024]{1,0:T(8,128)(2,1)}), bf16[256,1024]{1,0:T(8,128)(2,1)}) %reduce-scatter.7.cloned.1.call-update) | async-done | bytes 524304 | tf_op jit(solution)/shard_map/reduce_scatter | solution.py:54
  622.8 12.7 %sum_small.1 = f32[40,128]{1,0:T(8,128)} custom-call(f32[40,1024]{1,0:T(8,128)} %select_maximum_fusion.src), custom_call_target="tpu_custom_call" | custom-call | tf_op jit(solution)/shard_map/sum_small/pallas_call | solution.py:131
  642.1 5.4 reduce-scatter.13.cloned.1.call-done
  (261 shorter events, 111.1 us)
Async XLA Ops:
  7.2 73.7 %all-gather.5.cloned.1.call-start = ((), (), s32[]{:S(2)}) async-start(), calls=%async_computation.13 | async-start | bytes 2621440 | tf_op jit(solution)/shard_map/all_gather | solution.py:50
  20.8 118.6 %copy-start.26 = (f32[1024,1]{0,1:T(1,128)}, f32[1024,1]{0,1:T(1,128)S(1)}, u32[]{:S(2)}) copy-start(f32[1024,1]{0,1:T(1,128)S(1)} %get-tuple-element.130) | copy-start | bytes 12292
  23.6 113.1 %all-gather.7.cloned.1.call-start = ((), (), s32[]{:S(2)}) async-start(), calls=%async_computation.14 | async-start | bytes 2621440 | tf_op jit(solution)/shard_map/all_gather | solution.py:50
  24.3 144.7 %all-gather.9.cloned.1.call-start = ((), (), s32[]{:S(2)}) async-start(), calls=%async_computation.15 | async-start | bytes 2621440 | tf_op jit(solution)/shard_map/all_gather | solution.py:50
  27.0 26.8 %all-to-all-start = ((bf16[256,3,4,256]{0,3,1,2:T(8,128)(2,1)}), bf16[256,3,4,256]{0,3,1,2:T(8,128)(2,1)S(1)}, u32[]{:S(2)}, u32[]{:S(2)}) async-start(bf16[256,3,4,256]{0,3,1,2:T(8,128)(2,1)} %copy.156), calls=%async_computation | async-start | bytes 3145728 | tf_op jit(solution)/shard_map/all_to_all | solution.py:559
  30.8 111.2 %copy-start.32 = (f32[384]{0:T(512)}, f32[384]{0:T(512)S(1)}, u32[]{:S(2)}) copy-start(f32[384]{0:T(512)S(1)} %iota_convert_fusion) | copy-start | bytes 4612
  31.0 111.0 %copy-start.57 = (pred[256]{0:T(512)(128)(4,1)}, pred[256]{0:T(512)(128)(4,1)S(1)}, u32[]{:S(2)}) copy-start(pred[256]{0:T(512)(128)(4,1)S(1)} %broadcast_compare_fusion) | copy-start | bytes 772
  31.1 111.0 %copy-start.47 = (f32[256]{0:T(256)}, f32[256]{0:T(256)S(1)}, u32[]{:S(2)}) copy-start(f32[256]{0:T(256)S(1)} %add_add_fusion) | copy-start | bytes 3076
  53.8 25.8 %all-to-all-start.2 = ((bf16[8,4,12,1024]{3,1,2,0:T(4,128)(2,1)}), bf16[8,4,12,1024]{3,1,2,0:T(4,128)(2,1)S(1)}, u32[]{:S(2)}, u32[]{:S(2)}) async-start(bf16[8,4,12,1024]{3,1,2,0:T(4,128)(2,1)} %copy.162), calls=%async_computation.2 | async-start | bytes 1572864 | tf_op jit(solution)/shard_map/all_to_all | solution.py:546
  58.7 153.6 %all-gather.11.cloned.1.call-start = ((), (), s32[]{:S(2)}) async-start(), calls=%async_computation.16 | async-start | bytes 3932160 | tf_op jit(solution)/shard_map/all_gather | solution.py:547
  109.7 21.9 %all-to-all-start.1 = ((bf16[4,256,256]{1,2,0:T(8,128)(2,1)}), bf16[4,256,256]{1,2,0:T(8,128)(2,1)S(1)}, u32[]{:S(2)}, u32[]{:S(2)}) async-start(bf16[4,256,256]{1,2,0:T(8,128)(2,1)} %copy.159), calls=%async_computation.1 | async-start | bytes 1048576 | tf_op jit(solution)/shard_map/all_to_all | solution.py:62
  131.7 37.3 %all-to-all-start.3 = ((bf16[256,4,1024]{2,0,1:T(8,128)(2,1)}), bf16[256,4,1024]{2,0,1:T(8,128)(2,1)}, u32[]{:S(2)}, u32[]{:S(2)}) async-start(bf16[256,4,1024]{2,0,1:T(8,128)(2,1)} %bitcast.147), calls=%async_computation.3 | async-start | bytes 4194304 | tf_op jit(solution)/shard_map/all_to_all | solution.py:58
  377.2 12.4 %all-to-all-start.4 = ((bf16[256,4,256]{2,0,1:T(8,128)(2,1)}), bf16[256,4,256]{2,0,1:T(8,128)(2,1)S(1)}, u32[]{:S(2)}, u32[]{:S(2)}) async-start(bf16[256,4,256]{2,0,1:T(8,128)(2,1)} %bitcast.148), calls=%async_computation.4 | async-start | bytes 1048576 | tf_op jit(solution)/shard_map/all_to_all | solution.py:58
  380.7 93.3 %reduce-scatter.9.cloned.1.call-start = ((), (), s32[]{:S(2)}) async-start(), calls=%async_computation.18 | async-start | bytes 1769472 | tf_op jit(solution)/shard_map/reduce_scatter | solution.py:684
  431.6 69.2 %reduce-scatter.15.cloned.1.call-start = ((), (), s32[]{:S(2)}) async-start(), calls=%async_computation.21 | async-start | bytes 2359296 | tf_op jit(solution)/shard_map/reduce_scatter | solution.py:684
  437.6 100.1 %reduce-scatter.17.cloned.1.call-start = ((), (), s32[]{:S(2)}) async-start(), calls=%async_computation.22 | async-start | bytes 2359296 | tf_op jit(solution)/shard_map/reduce_scatter | solution.py:684
  443.9 138.0 %reduce-scatter.11.cloned.1.call-start = ((), (), s32[]{:S(2)}) async-start(), calls=%async_computation.19 | async-start | bytes 2359296 | tf_op jit(solution)/shard_map/reduce_scatter | solution.py:684
  446.9 173.6 %reduce-scatter.7.cloned.1.call-start = ((), (), s32[]{:S(2)}) async-start(), calls=%async_computation.17 | async-start | bytes 2621440 | tf_op jit(solution)/shard_map/reduce_scatter | solution.py:54
  476.0 8.9 %all-to-all-start.5 = ((bf16[128,3,1,256]{3,1,2,0:T(4,128)(2,1)}), bf16[128,3,1,256]{3,1,2,0:T(4,128)(2,1)S(1)}, u32[]{:S(2)}, u32[]{:S(2)}) async-start(bf16[128,3,1,256]{3,1,2,0:T(4,128)(2,1)} %copy.171), calls=%async_computation.7 | async-start | bytes 524288 | tf_op jit(solution)/shard_map/all_to_all | solution.py:694
  500.8 81.1 %all-to-all-start.6 = ((bf16[4,32,1024]{2,1,0:T(8,128)(2,1)}), bf16[4,32,1024]{2,1,0:T(8,128)(2,1)S(1)}, u32[]{:S(2)}, u32[]{:S(2)}) async-start(bf16[4,32,1024]{2,1,0:T(8,128)(2,1)} %bitcast.177), calls=%async_computation.11 | async-start | bytes 524288 | tf_op jit(solution)/shard_map/all_to_all | solution.py:62
  504.5 142.9 %reduce-scatter.13.cloned.1.call-start = ((), (), s32[]{:S(2)}) async-start(), calls=%async_computation.20 | async-start | bytes 327680 | tf_op jit(solution)/shard_map/reduce_scatter | solution.py:54
  537.7 45.1 %collective-permute-start = (bf16[128,1024]{1,0:T(8,128)(2,1)}, bf16[128,1024]{1,0:T(8,128)(2,1)S(1)}, u32[]{:S(2)}, u32[]{:S(2)}) collective-permute-start(bf16[128,1024]{1,0:T(8,128)(2,1)} %reduce-scatter.17.cloned.1.call-done), channel_id=1, source_target_pairs={{0,0},{4,1},{8,2},{12,3},{16,4},{20,5},{24,6},{28,7},{1,8},{5,9},{... | collective-permute-start | bytes 786440 | tf_op jit(solution)/shard_map/ppermute | solution.py:691
  539.3 81.2 %copy-start.3 = (bf16[256,1024]{1,0:T(8,128)(2,1)S(1)}, bf16[256,1024]{1,0:T(8,128)(2,1)}, u32[]{:S(2)}) copy-start(bf16[256,1024]{1,0:T(8,128)(2,1)} %param.14) | copy-start | bytes 1572868
  539.3 81.2 %copy-start.25 = (f32[1024,1]{0,1:T(1,128)S(1)}, f32[1024,1]{0,1:T(1,128)}, u32[]{:S(2)}) copy-start(f32[1024,1]{0,1:T(1,128)} %copy-done.24) | copy-start | bytes 12292
  (63 other events, 570.2 us)
Sparse Core Ops, SparseCore 0:
  23.7 46.7 all-gather.4
  72.3 35.1 all-gather.6
  109.3 58.0 all-gather.8
  169.1 43.1 all-gather.10
  431.8 32.4 reduce-scatter.8
  466.4 34.3 reduce-scatter.14
  503.1 34.5 reduce-scatter.16
  540.0 41.8 reduce-scatter.10
  584.9 35.6 reduce-scatter.6
  623.1 24.3 reduce-scatter.12

commit v3 on v2

--- a/solution.py
+++ b/solution.py
@@ -498,6 +498,292 @@
     )(slots, second, grad_all, grad_rows, w_in, w_out, small, sort, unsort, e_in, e_out)
 
 
+def tail_kernel(
+    heads, scaling, g_in, g_out, g_attn, d_heads, joined, lse, normed, qkv, source, gain, d_hidden, tiny,
+    d_source, o_in, o_out, o_qkv, o_attn, o_tiny, o_gain,
+    core_in, own, z_in, a_in, a_z, a_mine, gq, core_q, own_q, z_q, fin_in, fin_q,
+    dh, dj, acc_q, acc_k, acc_v, dn, dn_in, norm_v, qkv_v, tiny_e, tiny_m, tiny_c, late, late_e, late_m, late_c,
+    load_sem, core_sem, z_sem, cut_sem, te_sem, tc_sem,
+):
+    me, cut = lax.axis_index("expert"), lax.axis_index("cuts")
+    core, level = lax.rem(me, 2), lax.div(me, 2)
+    other = 1 - core
+    n_cuts, tokens, width = dh.shape
+    n_expert = tiny_e.shape[0]
+    levels = n_expert // 2
+    twin = (jnp.bitwise_xor(me, 1), cut)
+
+    def send(src, dst, sems, index, peer):
+        copy = pltpu.make_async_remote_copy(
+            src_ref=src, dst_ref=dst, send_sem=sems.at[0, index], recv_sem=sems.at[1, index],
+            device_id=peer, device_id_type=MESH,
+        )
+        copy.start()
+        return copy
+
+    def load(src, dst, index):
+        copy = pltpu.make_async_copy(src, dst, load_sem.at[index])
+        copy.start()
+        return copy
+
+    grads = (g_in, g_out, g_attn)
+    mine = [load(grads[m].at[:, core], own.at[m], m) for m in range(3)]
+    later = [load(normed, norm_v, 3), load(qkv, qkv_v, 4)]
+    barrier = pltpu.get_barrier_semaphore()
+    for k in range(1, n_expert):
+        pl.semaphore_signal(barrier, inc=1, device_id=(jnp.bitwise_xor(me, k), cut), device_id_type=MESH)
+    for k in range(1, n_cuts):
+        pl.semaphore_signal(barrier, inc=1, device_id=(me, jnp.bitwise_xor(cut, k)), device_id_type=MESH)
+    pl.semaphore_wait(barrier, n_expert + n_cuts - 2)
+
+    def columns(index, size):
+        return pl.ds(pl.multiple_of(index * size, size), size)
+
+    sent = []
+
+    def to_cuts(src_of, dst_of, base):
+        copies = []
+        for k in range(1, n_cuts):
+            peer = jnp.bitwise_xor(cut, k)
+            copies.append(send(src_of(peer), dst_of(k), cut_sem, base + k - 1, (me, peer)))
+        sent.extend(copies)
+        return copies
+
+    def to_levels(src_of, dst_of, base):
+        copies = []
+        for k in range(1, levels):
+            peer = jnp.bitwise_xor(level, k)
+            copies.append(send(src_of(peer), dst_of(k), z_sem, base + k - 1, (2 * peer + core, cut)))
+        sent.extend(copies)
+        return copies
+
+    def to_experts(src, dst, base):
+        copies = []
+        for k in range(1, n_expert):
+            peer = jnp.bitwise_xor(me, k)
+            copies.append(send(src.at[:, columns(peer, 128)], dst.at[k], te_sem, base + k - 1, (peer, cut)))
+        sent.extend(copies)
+        return copies
+
+    heads_moved = to_cuts(lambda peer: d_heads.at[:, columns(peer, width)], lambda k: dh.at[cut], 0)
+    twins = [send(grads[m].at[:, other], core_in.at[m], core_sem, m, twin) for m in range(3)]
+    tiny_moved = to_experts(tiny, tiny_e, 0)
+    dh[cut] = d_heads[:, columns(cut, width)]
+    z_moved = []
+    attn_moved = None
+    for m in range(3):
+        mine[m].wait()
+        twins[m].wait_recv()
+
+        @pl.loop(0, levels)
+        def _(step):
+            own[m, step] = (own[m, step].astype(F32) + core_in[m, step].astype(F32)).astype(BF)
+
+        if m < 2:
+            z_moved.append(to_levels(lambda peer: own.at[m, peer], lambda k: z_in.at[m, k - 1], 3 * m))
+        else:
+            piece = own.shape[2] // n_cuts
+            attn_moved = to_cuts(
+                lambda peer: own.at[2, :, columns(peer, piece)], lambda k: a_in.at[k - 1], 3
+            )
+
+    acc_q[...] = jnp.zeros_like(acc_q)
+    acc_k[...] = jnp.zeros_like(acc_k)
+    acc_v[...] = jnp.zeros_like(acc_v)
+    for copy in heads_moved:
+        copy.wait_recv()
+
+    @pl.loop(0, heads)
+    def _(head):
+        pair, half = lax.div(head, 2), lax.rem(head, 2)
+        lane = lax.broadcasted_iota(jnp.int32, (1, 128), 1)
+        keep = (lax.div(lane, HD) == half).astype(F32)
+        keep_low = keep.astype(BF)
+        cols = columns(pair, 128)
+        k_cols = pl.ds(pl.multiple_of(width + pair * 128, 128), 128)
+        v_cols = pl.ds(pl.multiple_of(2 * width + pair * 128, 128), 128)
+        for i in range(n_cuts):
+            reach = (i + 1) * tokens
+            here = pl.ds(i * tokens, tokens)
+            query = joined[here, cols] * keep_low
+            d_out = dh[i, :, cols] * keep_low
+            keys = joined[pl.ds(0, reach), k_cols]
+            scores = mm_nt(keys, query) * scaling - lse[head, :, here]
+            key_at = lax.broadcasted_iota(jnp.int32, scores.shape, 0)
+            query_at = lax.broadcasted_iota(jnp.int32, scores.shape, 1) + i * tokens
+            soft = jnp.exp(jnp.where(key_at <= query_at, scores, -1e30))
+            d_soft = mm_nt(joined[pl.ds(0, reach), v_cols], d_out)
+            delta = jnp.sum(soft * d_soft, axis=0, keepdims=True)
+            d_scores = (soft * (d_soft - delta)).astype(BF)
+            acc_v[pl.ds(0, reach), cols] += mm(soft.astype(BF), d_out)
+            acc_k[pl.ds(0, reach), cols] += mm(d_scores, query)
+            acc_q[here, cols] += mm_tn(d_scores, keys) * keep
+
+    dj[:, pl.ds(0, width)] = (acc_q[...] * scaling).astype(BF)
+    dj[:, pl.ds(width, width)] = (acc_k[...] * scaling).astype(BF)
+    dj[:, pl.ds(2 * width, width)] = acc_v[...].astype(BF)
+    for copy in later:
+        copy.wait()
+    dn_moved = []
+    for k in (3, 1, 2):
+        peer = jnp.bitwise_xor(cut, k)
+        dn[k] = mm_nt(dj[columns(peer, tokens), :], qkv_v[...]).astype(BF)
+        dn_moved.append(send(dn.at[k], dn_in.at[k - 1], cut_sem, 6 + k - 1, (me, peer)))
+    sent.extend(dn_moved)
+
+    @pl.loop(0, levels)
+    def _(step):
+        part = mm_tn(norm_v[:, columns(step, 256)], dj[...]).astype(BF)
+        gq[step] = part.reshape(2, 128, part.shape[1])
+
+    twins.append(send(gq.at[:, other], core_q, core_sem, 3, twin))
+    d_normed = mm_nt(dj[columns(cut, tokens), :], qkv_v[...])
+
+    for copy in attn_moved:
+        copy.wait_recv()
+    total = own[2, :, columns(cut, piece)].astype(F32)
+    for k in range(1, n_cuts):
+        total = total + a_in[k - 1].astype(F32)
+    a_mine[...] = total.astype(BF)
+    attn_z = to_levels(lambda peer: a_mine.at[peer], lambda k: a_z.at[k - 1], 9)
+
+    twins[3].wait_recv()
+
+    @pl.loop(0, levels)
+    def _(step):
+        own_q[step] = (gq[step, core].astype(F32) + core_q[step].astype(F32)).astype(BF)
+
+    qkv_z = to_levels(lambda peer: own_q.at[peer], lambda k: z_q.at[k - 1], 6)
+
+    for copy in tiny_moved:
+        copy.wait_recv()
+    small = tiny[:, columns(me, 128)]
+    for k in range(1, n_expert):
+        small = small + tiny_e[k]
+    tiny_m[...] = small
+
+    def tiny_cuts(src, dst, base):
+        copies = []
+        for k in range(1, n_cuts):
+            copies.append(send(src, dst.at[k], tc_sem, base + k - 1, (me, jnp.bitwise_xor(cut, k))))
+        sent.extend(copies)
+        return copies
+
+    tiny_last = tiny_cuts(tiny_m, tiny_c, 0)
+
+    for copy in z_moved[0]:
+        copy.wait_recv()
+    total = own[0, level].astype(F32)
+    for k in range(1, levels):
+        total = total + z_in[0, k - 1].astype(F32)
+    fin_in[...] = total.astype(BF).reshape(fin_in.shape)
+    in_last = to_cuts(lambda peer: fin_in.at[peer], lambda k: o_in.at[cut], 9)
+    o_in[cut] = fin_in[cut]
+
+    for copy in dn_moved:
+        copy.wait_recv()
+    for k in range(1, n_cuts):
+        d_normed = d_normed + dn_in[k - 1].astype(F32)
+    xhat, inv = norm_parts(source[...].astype(F32))
+    q = d_normed * gain[...]
+    mean_q = jnp.mean(q, axis=-1, keepdims=True)
+    mean_qx = jnp.mean(q * xhat, axis=-1, keepdims=True)
+    d_source[...] = d_hidden[...] + (q - mean_q - xhat * mean_qx) * inv
+    late[...] = jnp.broadcast_to(jnp.sum(d_normed * xhat, axis=0, keepdims=True), late.shape)
+    late_moved = to_experts(late, late_e, n_expert - 1)
+
+    for copy in tiny_last:
+        copy.wait_recv()
+    for k in range(1, n_cuts):
+        small = small + tiny_c[k]
+    o_tiny[...] = small
+
+    for copy in z_moved[1]:
+        copy.wait_recv()
+    total = own[1, level].astype(F32)
+    for k in range(1, levels):
+        total = total + z_in[1, k - 1].astype(F32)
+    o_out[...] = total.astype(BF)
+
+    for copy in late_moved:
+        copy.wait_recv()
+    small = late[:, columns(me, 128)]
+    for k in range(1, n_expert):
+        small = small + late_e[k]
+    late_m[...] = small
+    late_last = tiny_cuts(late_m, late_c, n_cuts - 1)
+
+    for copy in attn_z:
+        copy.wait_recv()
+    total = a_mine[level].astype(F32)
+    for k in range(1, levels):
+        total = total + a_z[k - 1].astype(F32)
+    o_attn[...] = total
+
+    for copy in qkv_z:
+        copy.wait_recv()
+    total = own_q[level].astype(F32)
+    for k in range(1, levels):
+        total = total + z_q[k - 1].astype(F32)
+    fin_q[...] = total.astype(BF).reshape(fin_q.shape)
+    qkv_last = to_cuts(lambda peer: fin_q.at[peer], lambda k: o_qkv.at[cut], 12)
+    o_qkv[cut] = fin_q[cut]
+
+    for copy in late_last:
+        copy.wait_recv()
+    for k in range(1, n_cuts):
+        small = small + late_c[k]
+    o_gain[...] = small
+    for copy in in_last + qkv_last:
+        copy.wait_recv()
+    for copy in sent + twins:
+        copy.wait_send()
+
+
+def tail(g_in, g_out, g_attn, d_heads, joined, lse, normed, qkv, source, gain, d_hidden, tiny, n_expert, n_cuts):
+    tokens, features = d_heads.shape
+    heads, seq_len = lse.shape
+    levels, own = n_expert // 2, features // n_cuts
+    deep = features // n_expert
+    piece, wide = deep // n_cuts, 3 * own
+    any_spec, vmem_spec = pl.BlockSpec(memory_space=pl.ANY), pl.BlockSpec(memory_space=pltpu.VMEM)
+    shape, vmem, dma = jax.ShapeDtypeStruct, pltpu.VMEM, pltpu.SemaphoreType.DMA
+    rows = tiny.shape[0]
+    grid = (levels, 2, deep, features)
+    return pl.pallas_call(
+        functools.partial(tail_kernel, heads, HD ** (-0.5)),
+        name="tail",
+        out_shape=(
+            shape((tokens, features), F32), shape((n_cuts, piece, features), BF), shape((deep, features), BF),
+            shape((n_cuts, piece, wide), BF), shape((piece, features), F32), shape((rows, 128), F32), shape((8, 128), F32),
+        ),
+        in_specs=[any_spec] * 3 + [vmem_spec] * 3 + [any_spec] * 2 + [vmem_spec] * 4,
+        out_specs=(vmem_spec,) * 7,
+        scratch_shapes=[
+            vmem((3, levels, deep, features), BF), vmem((3, levels, deep, features), BF),
+            vmem((2, levels - 1, deep, features), BF), vmem((n_cuts - 1, levels, piece, features), BF),
+            vmem((levels - 1, piece, features), BF), vmem((levels, piece, features), BF),
+            vmem((levels, 2, deep, wide), BF), vmem((levels, deep, wide), BF), vmem((levels, deep, wide), BF),
+            vmem((levels - 1, deep, wide), BF), vmem((n_cuts, piece, features), BF), vmem((n_cuts, piece, wide), BF),
+            vmem((n_cuts, tokens, own), BF), vmem((seq_len, wide), BF),
+            vmem((seq_len, own), F32), vmem((seq_len, own), F32), vmem((seq_len, own), F32),
+            vmem((n_cuts, tokens, features), BF), vmem((n_cuts - 1, tokens, features), BF),
+            vmem((seq_len, features), BF), vmem((features, wide), BF),
+            vmem((n_expert, rows, 128), F32), vmem((rows, 128), F32), vmem((n_cuts, rows, 128), F32),
+            vmem((8, features), F32), vmem((n_expert, 8, 128), F32), vmem((8, 128), F32), vmem((n_cuts, 8, 128), F32),
+            dma((5,)), dma((2, 4)), dma((2, 4 * (levels - 1))), dma((2, 5 * (n_cuts - 1))),
+            dma((2, 2 * (n_expert - 1))), dma((2, 2 * (n_cuts - 1))),
+        ],
+        compiler_params=pltpu.CompilerParams(
+            collective_id=2, has_side_effects=True, vmem_limit_bytes=48 << 20
+        ),
+        cost_estimate=pl.CostEstimate(flops=20_000_000_000, bytes_accessed=24 << 20, transcendentals=0),
+    )(
+        g_in.reshape(grid), g_out.reshape(grid), g_attn.reshape(grid), d_heads, joined, lse.reshape(heads, 1, seq_len),
+        normed, qkv, source, gain, d_hidden, tiny,
+    )
+
+
 def shards(
     block_input,
     routes,
@@ -665,7 +951,39 @@
     d_hidden = grad + d_hidden_norm
     d_attn = d_hidden.astype(BF)
     g_attn_out = mm_tn(head_out, d_attn)
-    d_heads = columns_to_cuts(mm_nt(d_attn, attn_full).astype(BF)).reshape(seq_len, heads, HD)
+    d_head_rows = mm_nt(d_attn, attn_full).astype(BF)
+    if fused:
+        tiny = jnp.concatenate([g_small, g_gain_two[None, :]], axis=0)
+        tiny = jnp.pad(tiny, ((0, -tiny.shape[0] % 8), (0, 0)))
+        d_block_input, s_in, s_out, s_qkv, s_attn_out, tiny, late = tail(
+            g_in.astype(BF), g_out.astype(BF), g_attn_out.astype(BF), d_head_rows, joined, log_norm[:, :, 0], normed,
+            qkv_here, block_input, gain_one[None, :], d_hidden, tiny, n_expert, n_cuts,
+        )
+        swap = [
+            ((flat % n_expert) * n_cuts + flat // n_expert, flat) for flat in range(n_expert * n_cuts)
+        ]
+        s_out = lax.ppermute(s_out, ("expert", "cuts"), swap).astype(F32)
+        s_in = s_in.swapaxes(0, 1).reshape(-1, w_in.shape[1]).astype(F32)
+        s_qkv = s_qkv.reshape(n_cuts, -1, 3, own).transpose(1, 2, 0, 3).reshape(-1, 3 * features).astype(F32)
+        width = features // (n_expert * n_cuts)
+        spot = lax.axis_index("cuts") * width
+        s_tiny = lax.dynamic_slice_in_dim(tiny, spot, width, axis=1)
+        s_late = lax.dynamic_slice_in_dim(late, spot, width, axis=1)
+        return (
+            block_out,
+            d_block_input,
+            s_qkv,
+            s_attn_out,
+            s_in,
+            s_out,
+            s_tiny[:experts_all].T,
+            s_tiny[experts_all : experts_all + 2].T,
+            s_late[0],
+            s_tiny[experts_all + 2],
+            g_expert_in,
+            g_expert_out,
+        )
+    d_heads = columns_to_cuts(d_head_rows).reshape(seq_len, heads, HD)
 
     soft_p = jnp.exp(masked_scores() - log_norm)
     d_soft = jnp.einsum("qhd,khd->hqk", d_heads, v_heads, preferred_element_type=F32)

time: 661 us -> 504 us (0.76)
  waiting for transfers between devices: 256 us -> 118 us
  Pallas kernels: 168 us -> 237 us
  matrix products: 100 us -> 49.8 us
  other arithmetic: 31 us -> 12.9 us
  starting transfers between devices: 30 us -> 17.8 us
    reduce_scatter x6 -> x0, waiting for transfers between devices: 133 us -> none  [the longest x4 90.3 us: over_experts(): lax.psum_scatter(part.astype(BF), 'expert', scatter_dimension=0, tiled=True)]
    pallas_call x1, Pallas kernels: 12.7 us -> 81.6 us  [tail(): pl.pallas_call(functools.partial(tail_kernel, heads, HD ** (-0.5)), name=...]
    dot_general x4 -> x0, matrix products: 28 us -> none  [the longest x1 13.1 us: shards(): jnp.einsum('qhd,khd->hqk', d_heads, v_heads, preferred_element_type=F32)]
    all_to_all x1, waiting for transfers between devices: 18.8 us -> 2.99 us  [to_owners(): lax.all_to_all(grid, 'expert', split_axis=0, concat_axis=2, tiled=True)]
    all_gather x3, waiting for transfers between devices: 0.04 us -> 13.5 us  [gather_cuts(): return lax.all_gather(rows, 'cuts', axis=0, tiled=True)]
    convert_element_type x4 -> x1, other arithmetic: 9.55 us -> 0.01 us  [shards(): gains = gather_cuts(jnp.stack([gain_attn, gain_ffn], axis=1)).astype(F32)]
    all_to_all x2 -> x1, waiting for transfers between devices: 34.3 us -> 24.9 us  [columns_to_cuts(): return lax.all_to_all(rows, 'cuts', split_axis=1, concat_axis=0, tiled=True)]
    all_to_all x2 -> x1, waiting for transfers between devices: 0.01 us -> 8.87 us  [rows_to_cuts(): return lax.all_to_all(rows, 'cuts', split_axis=0, concat_axis=1, tiled=True)]
  transfers between devices with their start and end apart: 18 -> 9, of which waited for: 11 -> 6; matrix products, arithmetic and copies ran while one was open for 15% -> 12% of each run, Pallas kernels for 2% -> 0%
where the time goes in v3:
time: 504 us; the launch traced here: 497 us
  Pallas kernels  237 us (47%)
  waiting for transfers between devices  118 us (23%)
  matrix products  49.8 us (10%)
  local copies, waits for them, and re-layouts  27.4 us (5%)
  blocking collectives  19.8 us (4%)
  starting transfers between devices  17.8 us (4%)
  between operations  14.8 us (3%)
  other arithmetic  12.9 us (3%)
    pallas_call x1, Pallas kernels, middle(): pl.pallas_call(functools.partial(middle_kernel, (n_expert, groups, here,...  155 us
    pallas_call x1, Pallas kernels, tail(): pl.pallas_call(functools.partial(tail_kernel, heads, HD ** (-0.5)), name=...  81.6 us
    all_gather x1, waiting for transfers between devices, to_owners(): return lax.all_gather(moved, 'cuts', axis=2, tiled=True)[0]  45.6 us
    all_to_all x1, waiting for transfers between devices, columns_to_cuts(): return lax.all_to_all(rows, 'cuts', split_axis=1, concat_axis=0, tiled=True)  24.9 us
    all_to_all x1, waiting for transfers between devices, shards(): lax.all_to_all(w_qkv.reshape(own, 3, n_cuts, own), 'cuts', split_axis=2,...  20.3 us
    all_gather x2, blocking collectives, gather_cuts(): return lax.all_gather(rows, 'cuts', axis=0, tiled=True)  19.8 us
    all_gather x3, waiting for transfers between devices, gather_cuts(): return lax.all_gather(rows, 'cuts', axis=0, tiled=True)  13.5 us
    dot_general x6, matrix products, mm_tn(): lax.dot_general(left, right, (((0,), (0,)), ((), ())), preferred_element_...  11.6 us
  transfers between devices with their start and end apart: 9, of which 6 were waited for; matrix products, arithmetic and copies ran while one was open for 12% of the time, Pallas kernels for 0%

profile of v3, /device:TPU:0, one launch (start us, length us, event | category | flops | bytes accessed | tf_op | source)
XLA Modules:
  0.0 497.1 jit_solution(10908855757036480346)
XLA Ops:
  11.2 9.6 %all_gather.18 = bf16[1024,2]{0,1:T(2,128)(2,1)S(1)} all-gather(bf16[256,2]{0,1:T(2,128)(2,1)S(1)} %pad_maximum_fusion.5), channel_id=1, replica_groups=mesh['expert'=8,'cuts'=4] {'cuts'}, dimensions={0}, use_global_device_ids=true | all-gather | bytes 5120 | tf_op jit(solution)/shard_map/all_gather | solution.py:50
  26.4 3.7 all-to-all-start
  32.9 20.3 %all-to-all-done = bf16[256,3,4,256]{0,3,1,2:T(8,128)(2,1)S(1)} async-done(((bf16[256,3,4,256]{0,3,1,2:T(8,128)(2,1)}), bf16[256,3,4,256]{0,3,1,2:T(8,128)(2,1)S(1)}, u32[]{:S(2)}, u32[]{:S(2)}) %all-to-all-start) | async-done | bytes 1572896 | tf_op jit(solution)/shard_map/all_to_all | solution.py:845
  53.2 4.9 all-to-all-start.2
  58.3 3.1 copy.148
  61.5 10.2 %all_gather.21 = bf16[1024,34]{1,0:T(8,128)(2,1)S(1)} all-gather(bf16[256,34]{1,0:T(8,128)(2,1)S(1)} %copy.125), channel_id=1, replica_groups=mesh['expert'=8,'cuts'=4] {'cuts'}, dimensions={0}, use_global_device_ids=true | all-gather | bytes 87040 | tf_op jit(solution)/shard_map/all_gather | solution.py:50
  76.0 3.0 all-to-all-done.2
  80.2 3.5 convolution_convert_fusion.1.joined
  85.4 4.6 fusion
  90.1 3.7 fusion.1
  93.8 5.0 %fusion.6 = bf16[1024,4,64]{0,2,1:T(8,128)(2,1)S(1)} fusion(f32[4,1024,1024]{1,2,0:T(8,128)S(1)} %get-tuple-element.134, f32[4,1024]{1,0:T(4,128)S(1)} %fusion.1, f32[4,1024]{1,0:T(4,128)S(1)} %get-tuple-element.133, pred[1024,1024]{0,1:T(8,128)(4,1)S(1)} %copy-done.15, bf16[1024,3,4,64]{0,3,2,1:T(8,128)(2,1)S(1)} %bitcast.129), kind=kOutput, calls=%fused_computation.27 | convolution fusion | flops 558104576 | bytes 18907136 | tf_op jit(solution)/shard_map/hqk,khd->qhd/dot_general | solution.py:863
  100.0 3.5 all-to-all-start.1
  105.1 8.9 %all-to-all-done.1 = bf16[4,256,256]{1,2,0:T(8,128)(2,1)S(1)} async-done(((bf16[4,256,256]{1,2,0:T(8,128)(2,1)}), bf16[4,256,256]{1,2,0:T(8,128)(2,1)S(1)}, u32[]{:S(2)}, u32[]{:S(2)}) %all-to-all-start.1) | async-done | bytes 524320 | tf_op jit(solution)/shard_map/all_to_all | solution.py:62
  114.0 5.0 %all-to-all-start.3 = ((bf16[256,4,1024]{2,0,1:T(8,128)(2,1)}), bf16[256,4,1024]{2,0,1:T(8,128)(2,1)}, u32[]{:S(2)}, u32[]{:S(2)}) async-start(bf16[256,4,1024]{2,0,1:T(8,128)(2,1)} %bitcast.113), calls=%async_computation.3 | async-start | bytes 4194304 | tf_op jit(solution)/shard_map/all_to_all | solution.py:58
  124.9 24.9 %all-to-all-done.3 = bf16[256,4,1024]{2,0,1:T(8,128)(2,1)} async-done(((bf16[256,4,1024]{2,0,1:T(8,128)(2,1)}), bf16[256,4,1024]{2,0,1:T(8,128)(2,1)}, u32[]{:S(2)}, u32[]{:S(2)}) %all-to-all-start.3) | async-done | bytes 2097184 | tf_op jit(solution)/shard_map/all_to_all | solution.py:58
  149.8 13.5 %all-gather.9.cloned.1.call-done = bf16[1024,1024]{1,0:T(8,128)(2,1)} async-done(((bf16[256,1024]{1,0:T(8,128)(2,1)}), bf16[1024,1024]{1,0:T(8,128)(2,1)}) %all-gather.9.cloned.1.call-update) | async-done | bytes 2097168 | tf_op jit(solution)/shard_map/all_gather | solution.py:50
  163.3 45.6 %all-gather.11.cloned.1.call-done = bf16[1,4,384,1024]{3,2,1,0:T(8,128)(2,1)} async-done(((bf16[1,4,96,1024]{3,2,1,0:T(8,128)(2,1)}), bf16[1,4,384,1024]{3,2,1,0:T(8,128)(2,1)}) %all-gather.11.cloned.1.call-update) | async-done | bytes 3145744 | tf_op jit(solution)/shard_map/all_gather | solution.py:833
  208.9 155.4 %middle.1 = (f32[2,256,1024]{2,1,0:T(8,128)}, bf16[2,2,8,24,1024]{4,3,2,1,0:T(8,128)(2,1)}, bf16[4,256,1024]{2,1,0:T(8,128)(2,1)}, bf16[4,256,1024]{2,1,0:T(8,12...) custom-call(bf16[2,8,24,1024]{3,2,1,0:T(8,128)(2,1)} %bitcast.130, ...), custom_call_target="tpu_custom_call" | custom-call | flops 21474836480 | bytes 50331648 | tf_op jit(solution)/shard_map/middle/pallas_call | solution.py:463
  366.2 2.9 fusion.12
  374.2 3.7 bitcast_convert_fusion.1
  378.0 3.7 bitcast_convert_fusion
  383.3 81.6 %tail.1 = (f32[256,1024]{1,0:T(8,128)S(1)}, bf16[4,32,1024]{2,1,0:T(8,128)(2,1)S(1)}, bf16[128,1024]{1,0:T(8,128)(2,1)S(1)}, bf16[4,32,768]{2,1,0:T(8,128)(2,1)S...) custom-call(bf16[4,2,128,1024]{3,2,1,0:T(8,128)(2,1)} %bitcast.146, ...), custom_call_target="tpu_custom_call" | custom-call | flops 20000000000 | bytes 25165824 | tf_op jit(solution)/shard_map/tail/pallas_call | solution.py:753
  466.4 8.8 %fusion.60 = f32[4,1024,1024]{2,1,0:T(8,128)} fusion(bf16[4,384,1024]{2,1,0:T(8,128)(2,1)S(1)} %copy-done.18, bf16[4,384,1024]{2,1,0:T(8,128)(2,1)S(1)} %copy-done.19), kind=kOutput, calls=%fused_computation.148 | convolution fusion | flops 3221225472 | bytes 23068672 | tf_op jit(solution)/shard_map/erd,erh->edh/dot_general | solution.py:901
  475.2 8.6 %fusion.61 = f32[4,1024,1024]{2,1,0:T(8,128)} fusion(bf16[4,384,1024]{2,1,0:T(8,128)(2,1)S(1)} %copy-done.17, bf16[4,384,1024]{2,1,0:T(8,128)(2,1)S(1)} %copy-done.16), kind=kOutput, calls=%fused_computation.149 | convolution fusion | flops 3221225472 | bytes 23068672 | tf_op jit(solution)/shard_map/erh,erd->ehd/dot_general | solution.py:900
  (182 shorter events, 44.8 us)
Async XLA Ops:
  7.2 17.3 %copy-start.20 = (bf16[256,3072]{1,0:T(8,128)(2,1)S(1)}, bf16[256,3072]{1,0:T(8,128)(2,1)}, u32[]{:S(2)}) copy-start(bf16[256,3072]{1,0:T(8,128)(2,1)} %param.17) | copy-start | bytes 4718596
  7.2 73.0 %all-gather.5.cloned.1.call-start = ((), (), s32[]{:S(2)}) async-start(), calls=%async_computation.4 | async-start | bytes 2621440 | tf_op jit(solution)/shard_map/all_gather | solution.py:50
  23.0 96.1 %all-gather.7.cloned.1.call-start = ((), (), s32[]{:S(2)}) async-start(), calls=%async_computation.5 | async-start | bytes 2621440 | tf_op jit(solution)/shard_map/all_gather | solution.py:50
  23.7 139.6 %all-gather.9.cloned.1.call-start = ((), (), s32[]{:S(2)}) async-start(), calls=%async_computation.6 | async-start | bytes 2621440 | tf_op jit(solution)/shard_map/all_gather | solution.py:50
  26.4 26.8 %all-to-all-start = ((bf16[256,3,4,256]{0,3,1,2:T(8,128)(2,1)}), bf16[256,3,4,256]{0,3,1,2:T(8,128)(2,1)S(1)}, u32[]{:S(2)}, u32[]{:S(2)}) async-start(bf16[256,3,4,256]{0,3,1,2:T(8,128)(2,1)} %copy.119), calls=%async_computation | async-start | bytes 3145728 | tf_op jit(solution)/shard_map/all_to_all | solution.py:845
  30.4 93.2 %copy-start.36 = (pred[256]{0:T(512)(128)(4,1)}, pred[256]{0:T(512)(128)(4,1)S(1)}, u32[]{:S(2)}) copy-start(pred[256]{0:T(512)(128)(4,1)S(1)} %broadcast_compare_fusion) | copy-start | bytes 772
  30.4 93.1 %copy-start.30 = (f32[256]{0:T(256)}, f32[256]{0:T(256)S(1)}, u32[]{:S(2)}) copy-start(f32[256]{0:T(256)S(1)} %add_add_fusion) | copy-start | bytes 3076
  31.0 27.2 %copy-start.27 = (bf16[256,32]{0,1:T(8,128)(2,1)S(1)}, bf16[256,32]{0,1:T(8,128)(2,1)}, u32[]{:S(2)}) copy-start(bf16[256,32]{0,1:T(8,128)(2,1)} %param.21) | copy-start | bytes 49156
  31.0 27.2 %copy-start.39 = (bf16[256,2]{0,1:T(2,128)(2,1)S(1)}, bf16[256,2]{0,1:T(2,128)(2,1)}, u32[]{:S(2)}) copy-start(bf16[256,2]{0,1:T(2,128)(2,1)} %param.22) | copy-start | bytes 3076
  53.2 25.8 %all-to-all-start.2 = ((bf16[8,4,12,1024]{3,1,2,0:T(4,128)(2,1)}), bf16[8,4,12,1024]{3,1,2,0:T(4,128)(2,1)S(1)}, u32[]{:S(2)}, u32[]{:S(2)}) async-start(bf16[8,4,12,1024]{3,1,2,0:T(4,128)(2,1)} %copy.127), calls=%async_computation.2 | async-start | bytes 1572864 | tf_op jit(solution)/shard_map/all_to_all | solution.py:832
  58.1 150.8 %all-gather.11.cloned.1.call-start = ((), (), s32[]{:S(2)}) async-start(), calls=%async_computation.7 | async-start | bytes 3932160 | tf_op jit(solution)/shard_map/all_gather | solution.py:833
  71.6 50.3 %copy-start.13 = (bf16[1024,34]{1,0:T(8,128)(2,1)}, bf16[1024,34]{1,0:T(8,128)(2,1)S(1)}, u32[]{:S(2)}) copy-start(bf16[1024,34]{1,0:T(8,128)(2,1)S(1)} %all_gather.21) | copy-start | bytes 208900
  100.0 14.0 %all-to-all-start.1 = ((bf16[4,256,256]{1,2,0:T(8,128)(2,1)}), bf16[4,256,256]{1,2,0:T(8,128)(2,1)S(1)}, u32[]{:S(2)}, u32[]{:S(2)}) async-start(bf16[4,256,256]{1,2,0:T(8,128)(2,1)} %copy.124), calls=%async_computation.1 | async-start | bytes 1048576 | tf_op jit(solution)/shard_map/all_to_all | solution.py:62
  114.0 35.8 %all-to-all-start.3 = ((bf16[256,4,1024]{2,0,1:T(8,128)(2,1)}), bf16[256,4,1024]{2,0,1:T(8,128)(2,1)}, u32[]{:S(2)}, u32[]{:S(2)}) async-start(bf16[256,4,1024]{2,0,1:T(8,128)(2,1)} %bitcast.113), calls=%async_computation.3 | async-start | bytes 4194304 | tf_op jit(solution)/shard_map/all_to_all | solution.py:58
  122.0 27.8 %copy-start.7 = (bf16[256,1024]{1,0:T(8,128)(2,1)}, bf16[256,1024]{1,0:T(8,128)(2,1)S(1)}, u32[]{:S(2)}) copy-start(bf16[256,1024]{1,0:T(8,128)(2,1)S(1)} %multiply_convert_fusion.second) | copy-start | bytes 1572868
  122.3 41.0 %copy-start.22 = (f32[256,34]{0,1:T(8,128)}, f32[256,34]{0,1:T(8,128)S(1)}, u32[]{:S(2)}) copy-start(f32[256,34]{0,1:T(8,128)S(1)} %fusion.59) | copy-start | bytes 104452
  122.3 86.6 %copy-start.28 = (f32[256]{0:T(256)}, f32[256]{0:T(256)S(1)}, u32[]{:S(2)}) copy-start(f32[256]{0:T(256)S(1)} %fusion.49) | copy-start | bytes 3076
  122.3 86.5 %copy-start.25 = (f32[256]{0:T(256)}, f32[256]{0:T(256)S(1)}, u32[]{:S(2)}) copy-start(f32[256]{0:T(256)S(1)} %slice_reduce_fusion) | copy-start | bytes 3076
  122.4 86.5 %copy-start.34 = (f32[256]{0:T(256)}, f32[256]{0:T(256)S(1)}, u32[]{:S(2)}) copy-start(f32[256]{0:T(256)S(1)} %fusion.37) | copy-start | bytes 3076
  383.3 83.1 %copy-start.18 = (bf16[4,384,1024]{2,1,0:T(8,128)(2,1)S(1)}, bf16[4,384,1024]{2,1,0:T(8,128)(2,1)}, u32[]{:S(2)}) copy-start(bf16[4,384,1024]{2,1,0:T(8,128)(2,1)} %get-tuple-element.42) | copy-start | bytes 9437188
  383.3 83.1 %copy-start.19 = (bf16[4,384,1024]{2,1,0:T(8,128)(2,1)S(1)}, bf16[4,384,1024]{2,1,0:T(8,128)(2,1)}, u32[]{:S(2)}) copy-start(bf16[4,384,1024]{2,1,0:T(8,128)(2,1)} %get-tuple-element.43) | copy-start | bytes 9437188
  465.7 22.2 %collective-permute-start = (bf16[128,1024]{1,0:T(8,128)(2,1)S(1)}, bf16[128,1024]{1,0:T(8,128)(2,1)S(1)}, u32[]{:S(2)}, u32[]{:S(2)}) collective-permute-start(bf16[128,1024]{1,0:T(8,128)(2,1)S(1)} %get-tuple-element.39), channel_id=1, source_target_pairs={{0,0},{4,1},{8,2},{12,3},{16,4},{20,5},{24,6},{28,7},{1,8},{5,9},{... | collective-permute-start | bytes 786440 | tf_op jit(solution)/shard_map/ppermute | solution.py:965
  466.4 8.8 %copy-start.16 = (bf16[4,384,1024]{2,1,0:T(8,128)(2,1)S(1)}, bf16[4,384,1024]{2,1,0:T(8,128)(2,1)}, u32[]{:S(2)}) copy-start(bf16[4,384,1024]{2,1,0:T(8,128)(2,1)} %get-tuple-element.45) | copy-start | bytes 9437188
  466.4 8.8 %copy-start.17 = (bf16[4,384,1024]{2,1,0:T(8,128)(2,1)S(1)}, bf16[4,384,1024]{2,1,0:T(8,128)(2,1)}, u32[]{:S(2)}) copy-start(bf16[4,384,1024]{2,1,0:T(8,128)(2,1)} %get-tuple-element.44) | copy-start | bytes 9437188
  (32 other events, 94.3 us)
Sparse Core Ops, SparseCore 0:
  23.1 47.6 all-gather.4
  72.6 41.1 all-gather.6
  115.7 47.5 all-gather.8
  165.0 43.8 all-gather.10
